TPU v7x, 256 devices: a whole 4x4x8 slice. The times are simulated.
256 devices in a mesh: gx: 2 (over core), gy: 16 (over y, x), gz: 8 (over z).
Axes of the slice: x: 4, y: 4, z: 8, core: 2. Of those that a mesh axis runs over, the one named last changes fastest.
Arguments:
- tokens: bfloat16 [2048, 8192], P('gy', ('gz', 'gx')), may hold values from -6 to 6
- gate_weight: bfloat16 [8192, 8192], P('gz', ('gx', 'gy')), may hold values from -0.0625 to 0.0625
- up_weight: bfloat16 [8192, 8192], P('gz', ('gx', 'gy')), may hold values from -0.0625 to 0.0625
- down_weight: bfloat16 [8192, 8192], P('gz', ('gx', 'gy')), may hold values from -0.0625 to 0.0625
- out_grad: bfloat16 [2048, 8192], P('gy', ('gz', 'gx')), may hold values from -6 to 6
Outputs:
- output: bfloat16 [2048, 8192], P('gy', ('gz', 'gx'))
- tokens_grad: bfloat16 [2048, 8192], P('gy', ('gz', 'gx'))
- gate_grad_w: float32 [8192, 8192], P('gz', ('gx', 'gy'))
- up_grad_w: float32 [8192, 8192], P('gz', ('gx', 'gy'))
- down_grad_w: float32 [8192, 8192], P('gz', ('gx', 'gy'))
All inputs are finite; a program needn't handle non-finite values.
Results may differ from a plain program's by a relative error of at most 0.023.
Values may be sent and summed in bfloat16 or wider, within the bound.
A program may use at most 128 MiB of HBM per device.

v0:
```python
import jax
import jax.numpy as jnp
from jax import lax
from jax.sharding import PartitionSpec as P


def dot_last(left, right):
    return lax.dot_general(
        left, right, (((1,), (1,)), ((), ())), preferred_element_type=jnp.float32
    )


def dot_first(left, right):
    return lax.dot_general(
        left, right, (((0,), (0,)), ((), ())), preferred_element_type=jnp.float32
    )


def add_block(piece, source):
    return dot_first(piece, source)


def per_device(tokens, gate_weight, up_weight, down_weight, out_grad):
    x_local = lax.all_gather(tokens, "gx", axis=1, tiled=True)
    gate_panel, up_panel, down_panel = (
        lax.all_gather(gate_weight, "gy", axis=1, tiled=True),
        lax.all_gather(up_weight, "gy", axis=1, tiled=True),
        lax.all_gather(down_weight, "gy", axis=1, tiled=True),
    )
    width = gate_panel.shape[1]
    row_block = x_local
    gate_part = jnp.dot(row_block, gate_panel, preferred_element_type=jnp.float32)
    up_part = jnp.dot(row_block, up_panel, preferred_element_type=jnp.float32)
    both_values = lax.psum_scatter(
        jnp.concatenate([gate_part, up_part], axis=1).astype(jnp.bfloat16),
        "gz",
        scatter_dimension=0,
        tiled=True,
    ).astype(jnp.float32)
    gate_value = both_values[:, :width]
    up_value = both_values[:, width:]
    activated = jax.nn.silu(gate_value)
    hidden = (activated * up_value).astype(jnp.bfloat16)
    hidden_block = lax.all_gather(hidden, "gz", axis=0, tiled=True)
    out_part = dot_last(hidden_block, down_panel)
    output = lax.psum_scatter(out_part.astype(jnp.bfloat16), "gx", scatter_dimension=1, tiled=True)
    grad_local = lax.all_gather(out_grad, "gx", axis=1, tiled=True)
    row_block = grad_local
    hidden_grad = lax.psum_scatter(
        jnp.dot(row_block, down_panel, preferred_element_type=jnp.float32).astype(jnp.bfloat16),
        "gz",
        scatter_dimension=0,
        tiled=True,
    ).astype(jnp.float32)
    sigmoid_gate = jax.nn.sigmoid(gate_value)
    gate_grad = (
        hidden_grad * up_value * sigmoid_gate * (1.0 + gate_value * (1.0 - sigmoid_gate))
    ).astype(jnp.bfloat16)
    up_grad = (hidden_grad * activated).astype(jnp.bfloat16)
    gate_block, up_block = (
        lax.all_gather(gate_grad, "gz", axis=0, tiled=True),
        lax.all_gather(up_grad, "gz", axis=0, tiled=True),
    )
    in_part = dot_last(gate_block, gate_panel) + dot_last(up_block, up_panel)
    tokens_grad = lax.psum_scatter(
        in_part.astype(jnp.bfloat16), "gx", scatter_dimension=1, tiled=True
    )
    gate_units, up_units, hidden_units = (
        lax.all_to_all(gate_block, "gy", split_axis=1, concat_axis=0, tiled=True),
        lax.all_to_all(up_block, "gy", split_axis=1, concat_axis=0, tiled=True),
        lax.all_to_all(hidden_block, "gy", split_axis=1, concat_axis=0, tiled=True),
    )
    piece = lax.all_gather(x_local, "gy", axis=0, tiled=True)
    gate_grad_w = add_block(piece, gate_units)
    up_grad_w = add_block(piece, up_units)
    down_grad_w = add_block(lax.all_gather(grad_local, "gy", axis=0, tiled=True), hidden_units)
    return (output, tokens_grad, gate_grad_w, up_grad_w, down_grad_w)


def solution(mesh):
    return jax.shard_map(
        per_device,
        mesh=mesh,
        in_specs=(
            P("gy", ("gz", "gx")),
            P("gz", ("gx", "gy")),
            P("gz", ("gx", "gy")),
            P("gz", ("gx", "gy")),
            P("gy", ("gz", "gx")),
        ),
        out_specs=(
            P("gy", ("gz", "gx")),
            P("gy", ("gz", "gx")),
            P("gz", ("gx", "gy")),
            P("gz", ("gx", "gy")),
            P("gz", ("gx", "gy")),
        ),
        check_vma=False,
    )
```

profile of v0, /device:TPU:1, one launch (start us, length us, event | category | flops | bytes accessed | tf_op | source)
XLA Modules:
  0.0 627.8 jit_solution(10019147761065522943)
XLA Ops:
  9.4 5.0 all_gather.30
  14.5 80.6 %all-gather.11.cloned.1.call-done = bf16[1024,4096]{1,0:T(8,128)(2,1)} async-done(((bf16[1024,256]{1,0:T(8,128)(2,1)}), bf16[1024,4096]{1,0:T(8,128)(2,1)}) %all-gather.11.cloned.1.call-update) | async-done | bytes 8388624 | tf_op jit(solution)/shard_map/all_gather | solution.py:27
  95.1 4.6 convolution_convert_fusion.1
  99.7 79.4 %all-gather.9.cloned.1.call-done = bf16[1024,4096]{1,0:T(8,128)(2,1)} async-done(((bf16[1024,256]{1,0:T(8,128)(2,1)}), bf16[1024,4096]{1,0:T(8,128)(2,1)}) %all-gather.9.cloned.1.call-update) | async-done | bytes 8388624 | tf_op jit(solution)/shard_map/all_gather | solution.py:26
  179.1 4.6 convolution_convert_fusion.2
  183.8 1.5 pad_maximum_fusion
  185.4 3.7 all_gather.35
  189.1 74.2 %all-gather.15.cloned.1.call-done = bf16[1024,4096]{1,0:T(8,128)(2,1)} async-done(((bf16[1024,256]{1,0:T(8,128)(2,1)}), bf16[1024,4096]{1,0:T(8,128)(2,1)}) %all-gather.15.cloned.1.call-update) | async-done | bytes 8388624 | tf_op jit(solution)/shard_map/all_gather | solution.py:28
  263.2 5.6 convolution_convert_fusion
  268.9 35.8 %reduce-scatter.5.cloned.1.call-done = bf16[16,8192]{1,0:T(8,128)(2,1)} async-done(((bf16[128,8192]{1,0:T(8,128)(2,1)}), bf16[16,8192]{1,0:T(8,128)(2,1)}) %reduce-scatter.5.cloned.1.call-update) | async-done | bytes 262160 | tf_op jit(solution)/shard_map/reduce_scatter | solution.py:34
  305.7 39.7 %reduce-scatter.9.cloned.1.call-done = bf16[16,4096]{1,0:T(8,128)(2,1)} async-done(((bf16[128,4096]{1,0:T(8,128)(2,1)}), bf16[16,4096]{1,0:T(8,128)(2,1)}) %reduce-scatter.9.cloned.1.call-update) | async-done | bytes 131088 | tf_op jit(solution)/shard_map/reduce_scatter | solution.py:49
  345.3 1.8 fusion.4
  350.0 34.2 %all-gather.17.cloned.1.call-done = bf16[128,4096]{1,0:T(8,128)(2,1)} async-done(((bf16[16,4096]{1,0:T(8,128)(2,1)}), bf16[128,4096]{1,0:T(8,128)(2,1)}) %all-gather.17.cloned.1.call-update) | async-done | bytes 1048592 | tf_op jit(solution)/shard_map/all_gather | solution.py:61
  384.1 2.4 copy.27
  386.5 6.5 %all-to-all-start = ((bf16[128,16,256]{2,0,1:T(8,128)(2,1)}), bf16[128,16,256]{2,0,1:T(8,128)(2,1)S(1)}, u32[]{:S(2)}, u32[]{:S(2)}) async-start(bf16[128,16,256]{2,0,1:T(8,128)(2,1)} %bitcast.44), calls=%async_computation.4 | async-start | bytes 2097152 | tf_op jit(solution)/shard_map/all_to_all | solution.py:69
  393.1 31.0 %all-gather.19.cloned.1.call-done = bf16[128,4096]{1,0:T(8,128)(2,1)} async-done(((bf16[16,4096]{1,0:T(8,128)(2,1)}), bf16[128,4096]{1,0:T(8,128)(2,1)}) %all-gather.19.cloned.1.call-update) | async-done | bytes 1048592 | tf_op jit(solution)/shard_map/all_gather | solution.py:62
  424.0 2.4 copy.26
  426.4 35.5 %all-gather.13.cloned.1.call-done = bf16[128,4096]{1,0:T(8,128)(2,1)} async-done(((bf16[16,4096]{1,0:T(8,128)(2,1)}), bf16[128,4096]{1,0:T(8,128)(2,1)}) %all-gather.13.cloned.1.call-update) | async-done | bytes 1048592 | tf_op jit(solution)/shard_map/all_gather | solution.py:44
  462.0 2.3 copy.25
  464.3 6.6 %all-to-all-start.1 = ((bf16[128,16,256]{2,0,1:T(8,128)(2,1)}), bf16[128,16,256]{2,0,1:T(8,128)(2,1)}, u32[]{:S(2)}, u32[]{:S(2)}) async-start(bf16[128,16,256]{2,0,1:T(8,128)(2,1)} %bitcast.43), calls=%async_computation.5 | async-start | bytes 2097152 | tf_op jit(solution)/shard_map/all_to_all | solution.py:70
  470.9 6.3 fusion.6
  477.2 7.1 %fusion = bf16[128,1024]{1,0:T(8,128)(2,1)} fusion(f32[128,1024]{1,0:T(8,128)S(1)} %fusion.6, bf16[128,4096]{1,0:T(8,128)(2,1)S(1)} %copy-done.3, bf16[1024,4096]{1,0:T(8,128)(2,1)} %all-gather.11.cloned.1.call-done), kind=kOutput, calls=%fused_computation.8 | convolution fusion | flops 1074003968 | bytes 10223616 | tf_op jit(solution)/shard_map/dot_general | solution.py:8
  484.3 6.6 %all-to-all-start.2 = ((bf16[128,16,256]{2,0,1:T(8,128)(2,1)}), bf16[128,16,256]{2,0,1:T(8,128)(2,1)S(1)}, u32[]{:S(2)}, u32[]{:S(2)}) async-start(bf16[128,16,256]{2,0,1:T(8,128)(2,1)} %bitcast.42), calls=%async_computation.6 | async-start | bytes 2097152 | tf_op jit(solution)/shard_map/all_to_all | solution.py:71
  491.2 7.0 %convolution_convert_fusion.3 = bf16[128,1024]{1,0:T(8,128)(2,1)} fusion(bf16[128,4096]{1,0:T(8,128)(2,1)S(1)} %copy-done.1, bf16[1024,4096]{1,0:T(8,128)(2,1)} %all-gather.15.cloned.1.call-done), kind=kOutput, calls=%fused_computation.9 | convolution fusion | flops 1073872896 | bytes 9699328 | tf_op jit(solution)/shard_map/dot_general | solution.py:8
  498.2 30.2 %all-gather.21.cloned.1.call-done = bf16[2048,1024]{1,0:T(8,128)(2,1)} async-done(((bf16[128,1024]{1,0:T(8,128)(2,1)}), bf16[2048,1024]{1,0:T(8,128)(2,1)}) %all-gather.21.cloned.1.call-update) | async-done | bytes 4194320 | tf_op jit(solution)/shard_map/all_gather | solution.py:73
  528.4 3.5 convolution_bitcast_fusion.2
  531.9 3.8 convolution_bitcast_fusion.1
  538.3 48.6 %all-gather.23.cloned.1.call-done = bf16[2048,1024]{1,0:T(8,128)(2,1)} async-done(((bf16[128,1024]{1,0:T(8,128)(2,1)}), bf16[2048,1024]{1,0:T(8,128)(2,1)}) %all-gather.23.cloned.1.call-update) | async-done | bytes 4194320 | tf_op jit(solution)/shard_map/all_gather | solution.py:76
  586.9 3.5 convolution_bitcast_fusion
  590.4 1.3 copy.18
  591.7 12.0 %reduce-scatter.11.cloned.1.call-done = bf16[128,512]{1,0:T(8,128)(2,1)} async-done(((bf16[128,1024]{1,0:T(8,128)(2,1)}), bf16[128,512]{1,0:T(8,128)(2,1)}) %reduce-scatter.11.cloned.1.call-update) | async-done | bytes 131088 | tf_op jit(solution)/shard_map/reduce_scatter | solution.py:65
  603.7 17.3 %reduce-scatter.7.cloned.1.call-done = bf16[128,512]{1,0:T(8,128)(2,1)} async-done(((bf16[128,1024]{1,0:T(8,128)(2,1)}), bf16[128,512]{1,0:T(8,128)(2,1)}) %reduce-scatter.7.cloned.1.call-update) | async-done | bytes 131088 | tf_op jit(solution)/shard_map/reduce_scatter | solution.py:46
  (42 shorter events, 9.0 us)
Async XLA Ops:
  7.2 87.9 %all-gather.11.cloned.1.call-start = ((), (), s32[]{:S(2)}) async-start(), calls=%async_computation.8 | async-start | bytes 8912896 | tf_op jit(solution)/shard_map/all_gather | solution.py:27
  7.9 171.2 %all-gather.9.cloned.1.call-start = ((), (), s32[]{:S(2)}) async-start(), calls=%async_computation.7 | async-start | bytes 8912896 | tf_op jit(solution)/shard_map/all_gather | solution.py:26
  8.6 254.6 %all-gather.15.cloned.1.call-start = ((), (), s32[]{:S(2)}) async-start(), calls=%async_computation.11 | async-start | bytes 8912896 | tf_op jit(solution)/shard_map/all_gather | solution.py:28
  9.4 295.3 %reduce-scatter.5.cloned.1.call-start = ((), (), s32[]{:S(2)}) async-start(), calls=%async_computation.9 | async-start | bytes 2359296 | tf_op jit(solution)/shard_map/reduce_scatter | solution.py:34
  14.5 169.3 %copy-start = (bf16[128,1024]{1,0:T(8,128)(2,1)}, bf16[128,1024]{1,0:T(8,128)(2,1)S(1)}, u32[]{:S(2)}) copy-start(bf16[128,1024]{1,0:T(8,128)(2,1)S(1)} %all_gather.30) | copy-start | bytes 786436
  99.7 85.7 %copy-start.5 = (bf16[128,512]{1,0:T(8,128)(2,1)S(1)}, bf16[128,512]{1,0:T(8,128)(2,1)}, u32[]{:S(2)}) copy-start(bf16[128,512]{1,0:T(8,128)(2,1)} %param.9) | copy-start | bytes 393220
  185.4 160.0 %reduce-scatter.9.cloned.1.call-start = ((), (), s32[]{:S(2)}) async-start(), calls=%async_computation.13 | async-start | bytes 1179648 | tf_op jit(solution)/shard_map/reduce_scatter | solution.py:49
  189.1 158.0 %copy-start.4 = (bf16[128,1024]{1,0:T(8,128)(2,1)}, bf16[128,1024]{1,0:T(8,128)(2,1)S(1)}, u32[]{:S(2)}) copy-start(bf16[128,1024]{1,0:T(8,128)(2,1)S(1)} %all_gather.35) | copy-start | bytes 786436
  268.9 115.2 %all-gather.17.cloned.1.call-start = ((), (), s32[]{:S(2)}) async-start(), calls=%async_computation.14 | async-start | bytes 1179648 | tf_op jit(solution)/shard_map/all_gather | solution.py:61
  347.1 76.9 %all-gather.19.cloned.1.call-start = ((), (), s32[]{:S(2)}) async-start(), calls=%async_computation.15 | async-start | bytes 1179648 | tf_op jit(solution)/shard_map/all_gather | solution.py:62
  347.9 114.1 %all-gather.13.cloned.1.call-start = ((), (), s32[]{:S(2)}) async-start(), calls=%async_computation.10 | async-start | bytes 1179648 | tf_op jit(solution)/shard_map/all_gather | solution.py:44
  348.6 179.8 %all-gather.21.cloned.1.call-start = ((), (), s32[]{:S(2)}) async-start(), calls=%async_computation.17 | async-start | bytes 4456448 | tf_op jit(solution)/shard_map/all_gather | solution.py:73
  349.4 237.5 %all-gather.23.cloned.1.call-start = ((), (), s32[]{:S(2)}) async-start(), calls=%async_computation.18 | async-start | bytes 4456448 | tf_op jit(solution)/shard_map/all_gather | solution.py:76
  384.1 86.8 %copy-start.2 = (bf16[128,4096]{1,0:T(8,128)(2,1)S(1)}, bf16[128,4096]{1,0:T(8,128)(2,1)}, u32[]{:S(2)}) copy-start(bf16[128,4096]{1,0:T(8,128)(2,1)} %all-gather.17.cloned.1.call-done) | copy-start | bytes 3145732
  386.5 77.7 %all-to-all-start = ((bf16[128,16,256]{2,0,1:T(8,128)(2,1)}), bf16[128,16,256]{2,0,1:T(8,128)(2,1)S(1)}, u32[]{:S(2)}, u32[]{:S(2)}) async-start(bf16[128,16,256]{2,0,1:T(8,128)(2,1)} %bitcast.44), calls=%async_computation.4 | async-start | bytes 2097152 | tf_op jit(solution)/shard_map/all_to_all | solution.py:69
  424.0 53.2 %copy-start.3 = (bf16[128,4096]{1,0:T(8,128)(2,1)S(1)}, bf16[128,4096]{1,0:T(8,128)(2,1)}, u32[]{:S(2)}) copy-start(bf16[128,4096]{1,0:T(8,128)(2,1)} %all-gather.19.cloned.1.call-done) | copy-start | bytes 3145732
  464.3 20.1 %all-to-all-start.1 = ((bf16[128,16,256]{2,0,1:T(8,128)(2,1)}), bf16[128,16,256]{2,0,1:T(8,128)(2,1)}, u32[]{:S(2)}, u32[]{:S(2)}) async-start(bf16[128,16,256]{2,0,1:T(8,128)(2,1)} %bitcast.43), calls=%async_computation.5 | async-start | bytes 2097152 | tf_op jit(solution)/shard_map/all_to_all | solution.py:70
  470.9 132.9 %reduce-scatter.11.cloned.1.call-start = ((), (), s32[]{:S(2)}) async-start(), calls=%async_computation.16 | async-start | bytes 393216 | tf_op jit(solution)/shard_map/reduce_scatter | solution.py:65
  477.2 14.0 %copy-start.1 = (bf16[128,4096]{1,0:T(8,128)(2,1)S(1)}, bf16[128,4096]{1,0:T(8,128)(2,1)}, u32[]{:S(2)}) copy-start(bf16[128,4096]{1,0:T(8,128)(2,1)} %all-gather.13.cloned.1.call-done) | copy-start | bytes 3145732
  484.3 102.6 %all-to-all-start.2 = ((bf16[128,16,256]{2,0,1:T(8,128)(2,1)}), bf16[128,16,256]{2,0,1:T(8,128)(2,1)S(1)}, u32[]{:S(2)}, u32[]{:S(2)}) async-start(bf16[128,16,256]{2,0,1:T(8,128)(2,1)} %bitcast.42), calls=%async_computation.6 | async-start | bytes 2097152 | tf_op jit(solution)/shard_map/all_to_all | solution.py:71
  490.9 130.0 %reduce-scatter.7.cloned.1.call-start = ((), (), s32[]{:S(2)}) async-start(), calls=%async_computation.12 | async-start | bytes 393216 | tf_op jit(solution)/shard_map/reduce_scatter | solution.py:46
Sparse Core Ops, SparseCore 0:
  10.4 84.6 all-gather.10
  97.5 81.6 all-gather.8
  181.6 81.6 all-gather.14
  265.6 39.0 reduce-scatter.4
  307.6 37.6 reduce-scatter.8
  347.6 36.5 all-gather.16
  386.5 37.4 all-gather.18
  425.8 36.1 all-gather.12
  465.0 63.4 all-gather.20
  530.7 56.1 all-gather.22
  590.0 13.6 reduce-scatter.10
  606.6 14.3 reduce-scatter.6
where the time goes:
time: 629 us; the launch traced here: 628 us
  waiting for transfers between devices  523 us (83%)
  matrix products  46 us (7%)
  starting transfers between devices  20.4 us (3%)
  between operations  14.3 us (2%)
  local copies, waits for them, and re-layouts  11 us (2%)
  blocking collectives  8.7 us (1%)
    all_gather x1, waiting for transfers between devices, per_device(): lax.all_gather(up_weight, 'gy', axis=1, tiled=True)  80.6 us
    all_gather x1, waiting for transfers between devices, per_device(): lax.all_gather(gate_weight, 'gy', axis=1, tiled=True)  79.4 us
    all_gather x1, waiting for transfers between devices, per_device(): lax.all_gather(down_weight, 'gy', axis=1, tiled=True)  74.2 us
    all_gather x1, waiting for transfers between devices, per_device(): lax.all_gather(grad_local, 'gy', axis=0, tiled=True)  48.6 us
    reduce_scatter x1, waiting for transfers between devices, per_device(): lax.psum_scatter(jnp.dot(row_block, down_panel, preferred_element_type=jn...  39.7 us
    reduce_scatter x1, waiting for transfers between devices, per_device(): lax.psum_scatter(jnp.concatenate([gate_part, up_part], axis=1).astype(jnp...  35.8 us
    all_gather x1, waiting for transfers between devices, per_device(): hidden_block = lax.all_gather(hidden, 'gz', axis=0, tiled=True)  35.5 us
    all_gather x1, waiting for transfers between devices, per_device(): lax.all_gather(gate_grad, 'gz', axis=0, tiled=True)  34.2 us
  transfers between devices with their start and end apart: 15, of which 12 were waited for; matrix products, arithmetic and copies ran while one was open for 9% of the time, Pallas kernels for 0%

commit v1 on v0

v1 whole, which is shorter than its diff:
```python
import jax
import jax.numpy as jnp
from jax import lax
from jax.sharding import PartitionSpec as P


def dot_last(left, right):
    return lax.dot_general(
        left, right, (((1,), (1,)), ((), ())), preferred_element_type=jnp.float32
    )


def dot_first(left, right):
    return lax.dot_general(
        left, right, (((0,), (0,)), ((), ())), preferred_element_type=jnp.float32
    )


def per_device(tokens, gate_weight, up_weight, down_weight, out_grad):
    x_half = lax.all_gather(tokens, "gy", axis=0, tiled=True)
    g_half = lax.all_gather(out_grad, "gy", axis=0, tiled=True)
    x_all = lax.all_gather(x_half, "gx", axis=1, tiled=True)
    g_all = lax.all_gather(g_half, "gx", axis=1, tiled=True)
    width = gate_weight.shape[1]
    both_weight = jnp.concatenate([gate_weight, up_weight], axis=1)
    both_part = jnp.dot(x_all, both_weight, preferred_element_type=jnp.float32)
    both_values = lax.psum_scatter(
        both_part.astype(jnp.bfloat16), "gz", scatter_dimension=0, tiled=True
    ).astype(jnp.float32)
    hidden_grad = lax.psum_scatter(
        jnp.dot(g_all, down_weight, preferred_element_type=jnp.float32).astype(jnp.bfloat16),
        "gz",
        scatter_dimension=0,
        tiled=True,
    ).astype(jnp.float32)
    gate_value = both_values[:, :width]
    up_value = both_values[:, width:]
    sigmoid_gate = jax.nn.sigmoid(gate_value)
    activated = gate_value * sigmoid_gate
    hidden = (activated * up_value).astype(jnp.bfloat16)
    gate_grad = (
        hidden_grad * up_value * sigmoid_gate * (1.0 + gate_value * (1.0 - sigmoid_gate))
    ).astype(jnp.bfloat16)
    up_grad = (hidden_grad * activated).astype(jnp.bfloat16)
    hidden_all = lax.all_gather(hidden, "gz", axis=0, tiled=True)
    grads_all = lax.all_gather(
        jnp.concatenate([gate_grad, up_grad], axis=1), "gz", axis=0, tiled=True
    )

    def scatter(part):
        pair = lax.psum_scatter(
            part.astype(jnp.bfloat16), "gx", scatter_dimension=1, tiled=True
        )
        return lax.psum_scatter(pair, "gy", scatter_dimension=0, tiled=True)

    output = scatter(dot_last(hidden_all, down_weight))
    tokens_grad = scatter(dot_last(grads_all, both_weight))
    both_grad_w = dot_first(x_all, grads_all)
    down_grad_w = dot_first(g_all, hidden_all)
    return (output, tokens_grad, both_grad_w[:, :width], both_grad_w[:, width:], down_grad_w)


def solution(mesh):
    return jax.shard_map(
        per_device,
        mesh=mesh,
        in_specs=(
            P("gy", ("gz", "gx")),
            P("gz", ("gx", "gy")),
            P("gz", ("gx", "gy")),
            P("gz", ("gx", "gy")),
            P("gy", ("gz", "gx")),
        ),
        out_specs=(
            P("gy", ("gz", "gx")),
            P("gy", ("gz", "gx")),
            P("gz", ("gx", "gy")),
            P("gz", ("gx", "gy")),
            P("gz", ("gx", "gy")),
        ),
        check_vma=False,
    )
```

time: 629 us -> 549 us (0.87)
  waiting for transfers between devices: 523 us -> 497 us
  starting transfers between devices: 20.4 us -> 0.66 us
  matrix products: 46 us -> 29.4 us
  blocking collectives: 8.7 us -> 0 us
  local copies, waits for them, and re-layouts: 11 us -> 4.15 us
    all_gather x8 -> x6, waiting for transfers between devices: 414 us -> 226 us  [the longest x1 53.9 us: per_device(): x_half = lax.all_gather(tokens, 'gy', axis=0, tiled=True)]
    reduce_scatter x4 -> x6, waiting for transfers between devices: 105 us -> 269 us  [the longest x2 154 us: scatter(): return lax.psum_scatter(pair, 'gy', scatter_dimension=0, tiled=True)]
    all_to_all x3 -> x0, starting transfers between devices: 19.7 us -> none  [the longest x1 6.6 us: per_device(): lax.all_to_all(hidden_block, 'gy', split_axis=1, concat_axis=0, tiled=True)]
    dot_general x3 -> x2, matrix products: 20.4 us -> 10.5 us  [dot_last(): lax.dot_general(left, right, (((1,), (1,)), ((), ())), preferred_element_...]
    all_gather x2 -> x0, blocking collectives: 8.7 us -> none  [the longest x1 5.04 us: per_device(): x_local = lax.all_gather(tokens, 'gx', axis=1, tiled=True)]
    all_to_all x3 -> x0, local copies, waits for them, and re-layouts: 7.08 us -> none  [the longest x1 2.39 us: per_device(): lax.all_to_all(gate_block, 'gy', split_axis=1, concat_axis=0, tiled=True)]
    dot_general x3 -> x2, matrix products: 14.9 us -> 10.4 us  [the longest x1 5.93 us: per_device(): both_part = jnp.dot(x_all, both_weight, preferred_element_type=jnp.float32)]
  transfers between devices with their start and end apart: 15 -> 12, of which waited for: 12 -> 12; matrix products, arithmetic and copies ran while one was open for 9% -> 6% of each run, Pallas kernels for 0% -> 0%
where the time goes in v1:
time: 549 us; the launch traced here: 548 us
  waiting for transfers between devices  497 us (91%)
  matrix products  29.4 us (5%)
  between operations  14.3 us (3%)
    reduce_scatter x2, waiting for transfers between devices, scatter(): return lax.psum_scatter(pair, 'gy', scatter_dimension=0, tiled=True)  154 us
    all_gather x1, waiting for transfers between devices, per_device(): x_half = lax.all_gather(tokens, 'gy', axis=0, tiled=True)  53.9 us
    all_gather x1, waiting for transfers between devices, per_device(): g_half = lax.all_gather(out_grad, 'gy', axis=0, tiled=True)  51.7 us
    all_gather x1, waiting for transfers between devices, per_device(): lax.all_gather(jnp.concatenate([gate_grad, up_grad], axis=1), 'gz', axis=...  44.7 us
    reduce_scatter x1, waiting for transfers between devices, per_device(): lax.psum_scatter(jnp.dot(g_all, down_weight, preferred_element_type=jnp.f...  39 us
    reduce_scatter x2, waiting for transfers between devices, scatter(): lax.psum_scatter(part.astype(jnp.bfloat16), 'gx', scatter_dimension=1, ti...  38.5 us
    all_gather x1, waiting for transfers between devices, per_device(): hidden_all = lax.all_gather(hidden, 'gz', axis=0, tiled=True)  37.6 us
    reduce_scatter x1, waiting for transfers between devices, per_device(): lax.psum_scatter(both_part.astype(jnp.bfloat16), 'gz', scatter_dimension=...  36.9 us
  transfers between devices with their start and end apart: 12, of which 12 were waited for; matrix products, arithmetic and copies ran while one was open for 6% of the time, Pallas kernels for 0%

profile of v1, /device:TPU:1, one launch (start us, length us, event | category | flops | bytes accessed | tf_op | source)
XLA Modules:
  0.0 548.5 jit_solution(4690731375221201113)
XLA Ops:
  7.2 0.7 all-gather.7.cloned.1.call-update
  8.0 0.7 all-gather.13.cloned.1.call-update
  8.7 53.9 %all-gather.7.cloned.1.call-done = bf16[2048,512]{1,0:T(8,128)(2,1)} async-done(((bf16[128,512]{1,0:T(8,128)(2,1)}), bf16[2048,512]{1,0:T(8,128)(2,1)}) %all-gather.7.cloned.1.call-update) | async-done | bytes 2097168 | tf_op jit(solution)/shard_map/all_gather | solution.py:20
  62.7 51.7 %all-gather.13.cloned.1.call-done = bf16[2048,512]{1,0:T(8,128)(2,1)} async-done(((bf16[128,512]{1,0:T(8,128)(2,1)}), bf16[2048,512]{1,0:T(8,128)(2,1)}) %all-gather.13.cloned.1.call-update) | async-done | bytes 2097168 | tf_op jit(solution)/shard_map/all_gather | solution.py:21
  114.6 22.4 %all-gather.9.cloned.1.call-done = bf16[2048,1024]{1,0:T(8,128)(2,1)} async-done(((bf16[2048,512]{1,0:T(8,128)(2,1)}), bf16[2048,1024]{1,0:T(8,128)(2,1)}) %all-gather.9.cloned.1.call-update) | async-done | bytes 4194320 | tf_op jit(solution)/shard_map/all_gather | solution.py:22
  136.9 5.9 %fusion = bf16[2048,512]{0,1:T(8,128)(2,1)} fusion(bf16[1024,512]{1,0:T(8,128)(2,1)S(1)} %constant_dynamic-update-slice_fusion, bf16[2048,1024]{1,0:T(8,128)(2,1)} %all-gather.9.cloned.1.call-done), kind=kOutput, calls=%fused_computation.3 | convolution fusion | flops 2148532224 | bytes 7340032 | tf_op jit(solution)/shard_map/dot_general | solution.py:26
  142.9 0.0 reduce-scatter.13.cloned.1.call-start
  142.9 16.0 %all-gather.15.cloned.1.call-done = bf16[2048,1024]{1,0:T(8,128)(2,1)} async-done(((bf16[2048,512]{1,0:T(8,128)(2,1)}), bf16[2048,1024]{1,0:T(8,128)(2,1)}) %all-gather.15.cloned.1.call-update) | async-done | bytes 4194320 | tf_op jit(solution)/shard_map/all_gather | solution.py:23
  158.9 4.5 convolution_convert_fusion.3
  163.4 0.0 all-gather.11.cloned.1.call-start
  163.4 36.9 %reduce-scatter.7.cloned.1.call-done = bf16[256,512]{0,1:T(8,128)(2,1)} async-done(((bf16[2048,512]{0,1:T(8,128)(2,1)}), bf16[256,512]{0,1:T(8,128)(2,1)}) %reduce-scatter.7.cloned.1.call-update) | async-done | bytes 262160 | tf_op jit(solution)/shard_map/reduce_scatter | solution.py:27
  200.3 1.0 convert_element_type.32
  201.3 39.0 %reduce-scatter.13.cloned.1.call-done = bf16[256,256]{0,1:T(8,128)(2,1)} async-done(((bf16[2048,256]{0,1:T(8,128)(2,1)}), bf16[256,256]{0,1:T(8,128)(2,1)}) %reduce-scatter.13.cloned.1.call-update) | async-done | bytes 131088 | tf_op jit(solution)/shard_map/reduce_scatter | solution.py:30
  240.3 1.7 fusion.3
  242.0 0.0 all-gather.17.cloned.1.call-start
  242.1 0.7 pad_maximum_fusion
  242.8 0.0 reduce-scatter.9.cloned.1.call-start
  242.9 37.6 %all-gather.11.cloned.1.call-done = bf16[2048,256]{0,1:T(8,128)(2,1)} async-done(((bf16[256,256]{0,1:T(8,128)(2,1)}), bf16[2048,256]{0,1:T(8,128)(2,1)}) %all-gather.11.cloned.1.call-update) | async-done | bytes 1048592 | tf_op jit(solution)/shard_map/all_gather | solution.py:45
  280.5 4.5 convolution_convert_fusion.1
  285.1 44.7 %all-gather.17.cloned.1.call-done = bf16[2048,512]{0,1:T(8,128)(2,1)} async-done(((bf16[256,512]{0,1:T(8,128)(2,1)}), bf16[2048,512]{0,1:T(8,128)(2,1)}) %all-gather.17.cloned.1.call-update) | async-done | bytes 2097168 | tf_op jit(solution)/shard_map/all_gather | solution.py:46
  329.8 5.9 %convolution_convert_fusion = bf16[2048,1024]{1,0:T(8,128)(2,1)} fusion(bf16[2048,512]{0,1:T(8,128)(2,1)} %all-gather.17.cloned.1.call-done, bf16[1024,512]{1,0:T(8,128)(2,1)S(1)} %constant_dynamic-update-slice_fusion), kind=kOutput, calls=%fused_computation | convolution fusion | flops 2149580800 | bytes 7340032 | tf_op jit(solution)/shard_map/dot_general | solution.py:8
  335.9 17.8 %reduce-scatter.9.cloned.1.call-done = bf16[2048,512]{1,0:T(8,128)(2,1)} async-done(((bf16[2048,1024]{1,0:T(8,128)(2,1)}), bf16[2048,512]{1,0:T(8,128)(2,1)}) %reduce-scatter.9.cloned.1.call-update) | async-done | bytes 2097168 | tf_op jit(solution)/shard_map/reduce_scatter | solution.py:51
  353.6 0.2 reduce-scatter.17.cloned.1.call-start
  353.9 20.8 %reduce-scatter.15.cloned.1.call-done = bf16[2048,512]{1,0:T(8,128)(2,1)} async-done(((bf16[2048,1024]{1,0:T(8,128)(2,1)}), bf16[2048,512]{1,0:T(8,128)(2,1)}) %reduce-scatter.15.cloned.1.call-update) | async-done | bytes 2097168 | tf_op jit(solution)/shard_map/reduce_scatter | solution.py:51
  374.7 3.4 convolution_bitcast_fusion.1
  378.1 1.3 copy.13
  379.4 5.1 convolution_bitcast_fusion
  384.6 0.1 fusion.6
  384.7 1.3 copy.12
  386.0 1.3 copy.11
  387.3 70.7 %reduce-scatter.11.cloned.1.call-done = bf16[128,512]{1,0:T(8,128)(2,1)} async-done(((bf16[2048,512]{1,0:T(8,128)(2,1)}), bf16[128,512]{1,0:T(8,128)(2,1)}) %reduce-scatter.11.cloned.1.call-update) | async-done | bytes 131088 | tf_op jit(solution)/shard_map/reduce_scatter | solution.py:54
  458.0 83.6 %reduce-scatter.17.cloned.1.call-done = bf16[128,512]{1,0:T(8,128)(2,1)} async-done(((bf16[2048,512]{1,0:T(8,128)(2,1)}), bf16[128,512]{1,0:T(8,128)(2,1)}) %reduce-scatter.17.cloned.1.call-update) | async-done | bytes 131088 | tf_op jit(solution)/shard_map/reduce_scatter | solution.py:54
  (27 shorter events, 0.5 us)
Async XLA Ops:
  7.2 151.7 %copy-start = (bf16[1024,256]{1,0:T(8,128)(2,1)S(1)}, bf16[1024,256]{1,0:T(8,128)(2,1)}, u32[]{:S(2)}) copy-start(bf16[1024,256]{1,0:T(8,128)(2,1)} %param.8) | copy-start | bytes 1572868
  7.2 107.3 %copy-start.2 = (bf16[1024,256]{1,0:T(8,128)(2,1)S(1)}, bf16[1024,256]{1,0:T(8,128)(2,1)}, u32[]{:S(2)}) copy-start(bf16[1024,256]{1,0:T(8,128)(2,1)} %param.6) | copy-start | bytes 1572868
  7.2 107.3 %copy-start.3 = (bf16[1024,256]{1,0:T(8,128)(2,1)S(1)}, bf16[1024,256]{1,0:T(8,128)(2,1)}, u32[]{:S(2)}) copy-start(bf16[1024,256]{1,0:T(8,128)(2,1)} %param.7) | copy-start | bytes 1572868
  7.2 55.4 %all-gather.7.cloned.1.call-start = ((), (), s32[]{:S(2)}) async-start(), calls=%async_computation.6 | async-start | bytes 2228224 | tf_op jit(solution)/shard_map/all_gather | solution.py:20
  7.9 106.5 %all-gather.13.cloned.1.call-start = ((), (), s32[]{:S(2)}) async-start(), calls=%async_computation.12 | async-start | bytes 2228224 | tf_op jit(solution)/shard_map/all_gather | solution.py:21
  8.7 128.2 %all-gather.9.cloned.1.call-start = ((), (), s32[]{:S(2)}) async-start(), calls=%async_computation.7 | async-start | bytes 6291456 | tf_op jit(solution)/shard_map/all_gather | solution.py:22
  62.6 96.3 %all-gather.15.cloned.1.call-start = ((), (), s32[]{:S(2)}) async-start(), calls=%async_computation.13 | async-start | bytes 6291456 | tf_op jit(solution)/shard_map/all_gather | solution.py:23
  114.4 85.9 %reduce-scatter.7.cloned.1.call-start = ((), (), s32[]{:S(2)}) async-start(), calls=%async_computation.8 | async-start | bytes 2359296 | tf_op jit(solution)/shard_map/reduce_scatter | solution.py:27
  142.9 97.4 %reduce-scatter.13.cloned.1.call-start = ((), (), s32[]{:S(2)}) async-start(), calls=%async_computation.14 | async-start | bytes 1179648 | tf_op jit(solution)/shard_map/reduce_scatter | solution.py:30
  163.4 117.1 %all-gather.11.cloned.1.call-start = ((), (), s32[]{:S(2)}) async-start(), calls=%async_computation.9 | async-start | bytes 1179648 | tf_op jit(solution)/shard_map/all_gather | solution.py:45
  242.0 87.8 %all-gather.17.cloned.1.call-start = ((), (), s32[]{:S(2)}) async-start(), calls=%async_computation.15 | async-start | bytes 2359296 | tf_op jit(solution)/shard_map/all_gather | solution.py:46
  242.8 110.8 %reduce-scatter.9.cloned.1.call-start = ((), (), s32[]{:S(2)}) async-start(), calls=%async_computation.10 | async-start | bytes 6291456 | tf_op jit(solution)/shard_map/reduce_scatter | solution.py:51
  285.1 89.6 %reduce-scatter.15.cloned.1.call-start = ((), (), s32[]{:S(2)}) async-start(), calls=%async_computation.16 | async-start | bytes 6291456 | tf_op jit(solution)/shard_map/reduce_scatter | solution.py:51
  335.8 38.9 %copy-start.1 = (bf16[2048,256]{0,1:T(8,128)(2,1)S(1)}, bf16[2048,256]{0,1:T(8,128)(2,1)}, u32[]{:S(2)}) copy-start(bf16[2048,256]{0,1:T(8,128)(2,1)} %all-gather.11.cloned.1.call-done) | copy-start | bytes 3145732
  335.8 122.2 %reduce-scatter.11.cloned.1.call-start = ((), (), s32[]{:S(2)}) async-start(), calls=%async_computation.11 | async-start | bytes 2228224 | tf_op jit(solution)/shard_map/reduce_scatter | solution.py:54
  353.6 188.0 %reduce-scatter.17.cloned.1.call-start = ((), (), s32[]{:S(2)}) async-start(), calls=%async_computation.17 | async-start | bytes 2228224 | tf_op jit(solution)/shard_map/reduce_scatter | solution.py:54
Sparse Core Ops, SparseCore 0:
  10.4 52.1 all-gather.6
  65.0 49.3 all-gather.12
  116.2 20.6 all-gather.8
  138.6 20.2 all-gather.14
  161.3 38.9 reduce-scatter.6
  203.3 36.9 reduce-scatter.12
  242.6 37.8 all-gather.10
  282.8 46.9 all-gather.16
  332.4 21.1 reduce-scatter.8
  356.0 18.5 reduce-scatter.14
  378.8 79.1 reduce-scatter.10
  462.0 79.6 reduce-scatter.16

commit v2 on v1

v2 whole, which is shorter than its diff:
```python
import jax
import jax.numpy as jnp
from jax import lax
from jax.experimental import pallas as pl
from jax.experimental.pallas import tpu as pltpu
from jax.sharding import PartitionSpec as P

MESH = pl.DeviceIdType.MESH
F32 = jnp.float32
BF16 = jnp.bfloat16


def dot_plain(left, right):
    return jnp.dot(left, right, preferred_element_type=F32)


def dot_last(left, right):
    return lax.dot_general(left, right, (((1,), (1,)), ((), ())), preferred_element_type=F32)


def dot_first(left, right):
    return lax.dot_general(left, right, (((0,), (0,)), ((), ())), preferred_element_type=F32)


def kernel(
    tok, wg, wu, wd, grd,
    out_ref, tg_ref, dg_ref, du_ref, dd_ref,
    act, w, rs_send, rs_recv, hall, gu, q, ps, pr, sa, ra, sb, rb, sc, rc,
    local_sem, s1, r1, s2, r2, s3, r3, sp, rp, zs, zr, as_, ar, pss, prs,
    sas, ras, sbs, rbs, scs, rcs,
):
    c = lax.axis_index("gx")
    gy = lax.axis_index("gy")
    z = lax.axis_index("gz")
    y, x = gy // 4, gy % 4
    f = x * (1 - c) + y * c
    s = y * (1 - c) + x * c
    fm, sm = 1 + 3 * c, 4 - 3 * c
    sg = 1 - 2 * c
    partner = (1 - c, gy, z)

    def gy_of(f_, s_):
        return ((f_ + 8) % 4) * fm + ((s_ + 8) % 4) * sm

    def at_fs(f_, s_):
        return (c, gy_of(f_, s_), z)

    def mod8(k):
        return (k + 16) % 8

    def at_z(k):
        return (c, gy, mod8(z + k))

    def rows_of(block):
        return pl.ds(pl.multiple_of(block * 128, 128), 128)

    def zrows(block):
        return pl.ds(pl.multiple_of(block * 256, 256), 256)

    sends = []

    def send(src, dst, ss, rs, device):
        copy = pltpu.make_async_remote_copy(
            src_ref=src, dst_ref=dst, send_sem=ss, recv_sem=rs,
            device_id=device, device_id_type=MESH,
        )
        copy.start()
        sends.append(copy)

    def recv(dst, ss, rs):
        pltpu.make_async_remote_copy(
            src_ref=dst, dst_ref=dst, send_sem=ss, recv_sem=rs,
            device_id=partner, device_id_type=MESH,
        ).wait_recv()

    barrier = pltpu.get_barrier_semaphore()
    peers = [
        at_fs(f + 1, s), at_fs(f + 2, s), at_fs(f + 3, s), at_fs(f, s + 1), at_fs(f, s + 3),
        at_z(1), at_z(-1), partner,
    ]
    for peer in peers:
        pl.semaphore_signal(barrier, inc=1, device_id=peer, device_id_type=MESH)

    own = [(tok, 0), (grd, 1)]
    locals_ = [
        pltpu.make_async_copy(wg, w.at[0], local_sem.at[0]),
        pltpu.make_async_copy(wu, w.at[1], local_sem.at[1]),
        pltpu.make_async_copy(wd, w.at[2], local_sem.at[2]),
        pltpu.make_async_copy(tok, act.at[0, c, rows_of(gy)], local_sem.at[3]),
        pltpu.make_async_copy(grd, act.at[1, c, rows_of(gy)], local_sem.at[4]),
    ]
    for copy in locals_:
        copy.start()
    pl.semaphore_wait(barrier, len(peers))

    def block(k, t):
        return gy_of(f - k, s + t)

    def act_block(a, k, t):
        return act.at[a, c, rows_of(block(k, t))]

    def to_partner(a, k, t, src=None):
        ref = act_block(a, k, t)
        send(ref if src is None else src, ref, sp.at[a, 4 * t + k], rp.at[a, 4 * t + k], partner)

    def gather_own(a):
        src = own[a][0]
        ref = act_block(a, 0, 0)
        for k in (1, 3, 2):
            send(src, ref, s1.at[a, k], r1.at[a, k], at_fs(f + k, s))
        send(src, ref, s2.at[a, 0, 0], r2.at[a, 0, 0], at_fs(f, s + 1))
        send(src, ref, s2.at[a, 1, 0], r2.at[a, 1, 0], at_fs(f, s + 3))
        to_partner(a, 0, 0, src)

    def gather_row(a):
        for k in (1, 3, 2):
            ref = act_block(a, k, 0)
            recv(ref, s1.at[a, k], r1.at[a, k])
            send(ref, ref, s2.at[a, 0, k], r2.at[a, 0, k], at_fs(f, s + 1))
            send(ref, ref, s2.at[a, 1, k], r2.at[a, 1, k], at_fs(f, s + 3))
            to_partner(a, k, 0)

    def gather_near(a):
        for k in (0, 1, 3, 2):
            for way, t in ((0, 3), (1, 1)):
                ref = act_block(a, k, t)
                recv(ref, s2.at[a, way, k], r2.at[a, way, k])
                if way == 0 and k < 2:
                    send(ref, ref, s3.at[a, k], r3.at[a, k], at_fs(f, s + 1))
                if way == 1 and k >= 2:
                    send(ref, ref, s3.at[a, k], r3.at[a, k], at_fs(f, s + 3))
                to_partner(a, k, t)

    def gather_far(a):
        for k in (0, 3, 1, 2):
            ref = act_block(a, k, 2)
            recv(ref, s3.at[a, k], r3.at[a, k])
            to_partner(a, k, 2)

    def gather_end(a):
        for t in (0, 3, 1, 2):
            for k in range(4):
                ref = act.at[a, 1 - c, rows_of(gy_of(f + t, s - k))]
                recv(ref, sp.at[a, 4 * t + k], rp.at[a, 4 * t + k])
        locals_[3 + a].wait()

    def part(a, d):
        rows = zrows(d)
        source = 0 if a < 2 else 1
        return dot_plain(act[source, 0, rows, :], w[a, 0:512, :]) + dot_plain(
            act[source, 1, rows, :], w[a, 512:1024, :]
        )

    def sum_step(arrays, j):
        for a in arrays:
            for base, last, d, to in (
                (0, 4, z - sg * (4 - j), -sg), (4, 3, z + sg * (3 - j), sg)
            ):
                if j >= last:
                    continue
                value = part(a, mod8(d))
                if j > 0:
                    recv(rs_recv.at[a, base + j - 1], zs.at[a, base + j - 1], zr.at[a, base + j - 1])
                    value = value + rs_recv[a, base + j - 1].astype(F32)
                rs_send[a, base + j] = value.astype(BF16)
                send(
                    rs_send.at[a, base + j], rs_recv.at[a, base + j],
                    zs.at[a, base + j], zr.at[a, base + j], at_z(to),
                )

    def sum_end(a):
        value = part(a, z)
        for slot in (3, 6):
            recv(rs_recv.at[a, slot], zs.at[a, slot], zr.at[a, slot])
            value = value + rs_recv[a, slot].astype(F32)
        return value

    def zrecv(t, slot, b):
        recv(hall.at[t, zrows(b)], as_.at[t, slot], ar.at[t, slot])

    def zgather(t, j):
        for base, last, way in ((0, 4, sg), (4, 3, -sg)):
            b = mod8(z + way * j)
            if j > 0 and j <= last:
                zrecv(t, base + j - 1, b)
            if j < last:
                ref = hall.at[t, zrows(b)]
                send(ref, ref, as_.at[t, base + j], ar.at[t, base + j], at_z(-way))

    def product(o, b, half):
        rows = zrows(b)
        cols = pl.ds(pl.multiple_of(half * 512, 512), 512)
        if o == 0:
            return dot_last(hall[0, rows, :], w[2, cols, :])
        return dot_last(hall[1, rows, :], w[0, cols, :]) + dot_last(hall[2, rows, :], w[1, cols, :])

    def out_block(o, b):
        rows = zrows(b)
        ps[o, rows, :] = product(o, b, 1 - c).astype(BF16)
        send(ps.at[o, rows], pr.at[o, rows], pss.at[o, b], prs.at[o, b], partner)
        q[o, rows, :] = product(o, b, c)

    def out_pair_end(o):
        for b in range(8):
            recv(pr.at[o, zrows(b)], pss.at[o, b], prs.at[o, b])

    def chip_sum(o, k, t):
        rows = rows_of(gy_of(f + k, s + t))
        return q[o, rows, :] + pr[o, rows, :].astype(F32)

    def stage_a(o):
        for k in (0, 2, 1, 3):
            sa[o, k] = chip_sum(o, k, 2).astype(BF16)
            send(sa.at[o, k], ra.at[o, k], sas.at[o, k], ras.at[o, k], at_fs(f, s + (1 if k < 2 else 3)))

    def stage_b(o):
        for k in (2, 3, 0, 1):
            for way, t, kk in ((0, 1, k), (1, 3, (k + 2) % 4)):
                value = chip_sum(o, kk, t)
                if (way == 0) == (kk < 2):
                    recv(ra.at[o, kk], sas.at[o, kk], ras.at[o, kk])
                    value = value + ra[o, kk].astype(F32)
                sb[o, 4 * way + kk] = value.astype(BF16)
                send(
                    sb.at[o, 4 * way + kk], rb.at[o, 4 * way + kk],
                    sbs.at[o, 4 * way + kk], rbs.at[o, 4 * way + kk], at_fs(f, s + t),
                )

    def stage_c(o):
        for k in (2, 3, 1, 0):
            value = chip_sum(o, k, 0)
            for way in range(2):
                slot = 4 * way + k
                recv(rb.at[o, slot], sbs.at[o, slot], rbs.at[o, slot])
                value = value + rb[o, slot].astype(F32)
            if k > 0:
                sc[o, k] = value.astype(BF16)
                send(sc.at[o, k], rc.at[o, k], scs.at[o, k], rcs.at[o, k], at_fs(f + k, s))
            else:
                q[o, rows_of(gy), :] = value

    def stage_d(o, ref):
        value = q[o, rows_of(gy), :]
        for k in (1, 3, 2):
            recv(rc.at[o, k], scs.at[o, k], rcs.at[o, k])
            value = value + rc[o, k].astype(F32)
        ref[...] = value.astype(BF16)

    def weight_grad(ref, a, t):
        for half in range(2):
            ref[half * 512:(half + 1) * 512, :] = dot_first(act[a, half], hall[t])

    gather_own(0)
    gather_row(0)
    gather_own(1)
    gather_near(0)
    gather_row(1)
    gather_far(0)
    for copy in locals_[:3]:
        copy.wait()
    gather_end(0)
    sum_step((0, 1), 0)
    gather_near(1)
    sum_step((0, 1), 1)
    gather_far(1)
    sum_step((0, 1), 2)
    gather_end(1)
    sum_step((2,), 0)
    sum_step((0, 1), 3)
    sum_step((2,), 1)
    gate = sum_end(0)
    up = sum_end(1)
    gu[0] = gate
    gu[1] = up
    sigmoid = jax.nn.sigmoid(gate)
    hall[0, zrows(z), :] = (gate * sigmoid * up).astype(BF16)
    zgather(0, 0)
    sum_step((2,), 2)
    out_block(0, z)
    sum_step((2,), 3)
    zgather(0, 1)
    out_block(0, mod8(z + 1))
    out_block(0, mod8(z - 1))
    hidden_grad = sum_end(2)
    gate = gu[0]
    up = gu[1]
    sigmoid = jax.nn.sigmoid(gate)
    hall[1, zrows(z), :] = (
        hidden_grad * up * sigmoid * (1.0 + gate * (1.0 - sigmoid))
    ).astype(BF16)
    zgather(1, 0)
    hall[2, zrows(z), :] = (hidden_grad * (gate * sigmoid)).astype(BF16)
    zgather(2, 0)
    zgather(0, 2)
    out_block(0, mod8(z + 2))
    out_block(0, mod8(z - 2))
    zgather(0, 3)
    out_block(0, mod8(z + 3))
    zgather(1, 1)
    zgather(2, 1)
    out_block(0, mod8(z - 3))
    zrecv(0, 3, mod8(z + 4 * sg))
    out_block(0, mod8(z + 4))
    out_block(1, z)
    out_pair_end(0)
    stage_a(0)
    out_block(1, mod8(z + 1))
    out_block(1, mod8(z - 1))
    zgather(1, 2)
    zgather(2, 2)
    stage_b(0)
    out_block(1, mod8(z + 2))
    out_block(1, mod8(z - 2))
    zgather(1, 3)
    zgather(2, 3)
    stage_c(0)
    out_block(1, mod8(z + 3))
    out_block(1, mod8(z - 3))
    weight_grad(dd_ref, 1, 0)
    stage_d(0, out_ref)
    zrecv(1, 3, mod8(z + 4 * sg))
    zrecv(2, 3, mod8(z + 4 * sg))
    out_block(1, mod8(z + 4))
    out_pair_end(1)
    stage_a(1)
    stage_b(1)
    weight_grad(dg_ref, 0, 1)
    stage_c(1)
    weight_grad(du_ref, 0, 2)
    stage_d(1, tg_ref)
    for copy in sends:
        copy.wait_send()


def per_device(tokens, gate_weight, up_weight, down_weight, out_grad):
    dma = pltpu.SemaphoreType.DMA
    vmem = pltpu.VMEM
    return pl.pallas_call(
        kernel,
        out_shape=(
            jax.ShapeDtypeStruct((128, 512), BF16),
            jax.ShapeDtypeStruct((128, 512), BF16),
            jax.ShapeDtypeStruct((1024, 256), F32),
            jax.ShapeDtypeStruct((1024, 256), F32),
            jax.ShapeDtypeStruct((1024, 256), F32),
        ),
        in_specs=[pl.BlockSpec(memory_space=pl.ANY)] * 5,
        out_specs=tuple([pl.BlockSpec(memory_space=pltpu.VMEM)] * 5),
        scratch_shapes=[
            vmem((2, 2, 2048, 512), BF16),
            vmem((3, 1024, 256), BF16),
            vmem((3, 7, 256, 256), BF16),
            vmem((3, 7, 256, 256), BF16),
            vmem((3, 2048, 256), BF16),
            vmem((2, 256, 256), F32),
            vmem((2, 2048, 512), F32),
            vmem((2, 2048, 512), BF16),
            vmem((2, 2048, 512), BF16),
            vmem((2, 4, 128, 512), BF16),
            vmem((2, 4, 128, 512), BF16),
            vmem((2, 8, 128, 512), BF16),
            vmem((2, 8, 128, 512), BF16),
            vmem((2, 4, 128, 512), BF16),
            vmem((2, 4, 128, 512), BF16),
            dma((5,)),
            dma((2, 4)), dma((2, 4)),
            dma((2, 2, 4)), dma((2, 2, 4)),
            dma((2, 4)), dma((2, 4)),
            dma((2, 16)), dma((2, 16)),
            dma((3, 7)), dma((3, 7)),
            dma((3, 7)), dma((3, 7)),
            dma((2, 8)), dma((2, 8)),
            dma((2, 4)), dma((2, 4)),
            dma((2, 8)), dma((2, 8)),
            dma((2, 4)), dma((2, 4)),
        ],
        compiler_params=pltpu.CompilerParams(
            collective_id=0, has_side_effects=True, vmem_limit_bytes=60 * 1024 * 1024
        ),
        name="slab",
    )(tokens, gate_weight, up_weight, down_weight, out_grad)


def solution(mesh):
    return jax.shard_map(
        per_device,
        mesh=mesh,
        in_specs=(
            P("gy", ("gz", "gx")),
            P("gz", ("gx", "gy")),
            P("gz", ("gx", "gy")),
            P("gz", ("gx", "gy")),
            P("gy", ("gz", "gx")),
        ),
        out_specs=(
            P("gy", ("gz", "gx")),
            P("gy", ("gz", "gx")),
            P("gz", ("gx", "gy")),
            P("gz", ("gx", "gy")),
            P("gz", ("gx", "gy")),
        ),
        check_vma=False,
    )
```

time: 549 us -> 131 us (0.24)
  waiting for transfers between devices: 497 us -> 0 us
  Pallas kernels: 0 us -> 123 us
  matrix products: 29.4 us -> 0 us
  between operations: 14.3 us -> 0.65 us
    reduce_scatter x6 -> x0, waiting for transfers between devices: 269 us -> none  [the longest x2 154 us: scatter(): return lax.psum_scatter(pair, 'gy', scatter_dimension=0, tiled=True)]
    all_gather x6 -> x0, waiting for transfers between devices: 226 us -> none  [the longest x1 53.9 us: per_device(): x_half = lax.all_gather(tokens, 'gy', axis=0, tiled=True)]
    pallas_call x0 -> x1, Pallas kernels: none -> 123 us  [per_device(): pl.pallas_call(kernel, out_shape=(jax.ShapeDtypeStruct((128, 512), BF16),...]
    dot_general x6 -> x0, matrix products: 29.4 us -> none  [the longest x2 10.5 us: dot_last(): lax.dot_general(left, right, (((1,), (1,)), ((), ())), preferred_element_...]
  transfers between devices with their start and end apart: 12 -> 0, of which waited for: 12 -> 0; matrix products, arithmetic and copies ran while one was open for 6% -> 0% of each run, Pallas kernels for 0% -> 0%
where the time goes in v2:
time: 131 us
  Pallas kernels  123 us (94%)
  local copies, waits for them, and re-layouts  7.19 us (5%)
    pallas_call x1, Pallas kernels, per_device(): pl.pallas_call(kernel, out_shape=(jax.ShapeDtypeStruct((128, 512), BF16),...  123 us
    unnamed x11, local copies, waits for them, and re-layouts  7.19 us

profile of v2, /device:TPU:1, one launch (start us, length us, event | category | flops | bytes accessed | tf_op | source)
XLA Modules:
  0.0 130.6 jit_solution(12211262308528694631)
XLA Ops:
  0.6 122.8 %slab.1 = (bf16[128,512]{1,0:T(8,128)(2,1)}, bf16[128,512]{1,0:T(8,128)(2,1)}, f32[1024,256]{1,0:T(8,128)}, f32[1024,256]{1,0:T(8,128)}, f32[1024,256]{1,0:T(8,128)}) custom-call(bf16[128,512]{1,0:T(8,128)(2,1)} %tok.1, bf16[1024,256]{1,0:T(8,128)(2,1)} %wg.1, bf16[1024,256]{1,0:T(8,128)(2,1)} %wu.1, bf16[1024,256]{1,0:T(8,128)(2,1)} %wd.1, bf16[128,512]{1,0:T(8,128)(2,1)} %grd.1), custom_call_target="tpu_custom_call" | custom-call | tf_op jit(solution)/shard_map/slab/pallas_call | solution.py:338
  123.4 0.0 copy-start.2
  123.4 1.6 %copy.15 = bf16[128,512]{1,0:T(8,128)(2,1)} copy(bf16[128,512]{1,0:T(8,128)(2,1)} %get-tuple-element.10) | data formatting | bytes 262144
  125.0 0.0 copy-done.2
  125.0 0.7 copy.16
  125.7 0.0 copy-start.1
  125.7 2.4 %copy.17 = f32[1024,256]{1,0:T(8,128)} copy(f32[1024,256]{1,0:T(8,128)} %get-tuple-element.12) | data formatting | bytes 2097152
  128.0 0.0 copy-done.1
  128.0 0.0 copy-start
  128.0 1.0 copy.18
  129.0 0.6 copy-done
  129.6 1.0 copy.19
Async XLA Ops:
  123.4 1.6 %copy-start.2 = (bf16[128,512]{1,0:T(8,128)(2,1)S(1)}, bf16[128,512]{1,0:T(8,128)(2,1)}, u32[]{:S(2)}) copy-start(bf16[128,512]{1,0:T(8,128)(2,1)} %get-tuple-element.11) | copy-start | bytes 393220
  125.7 2.4 %copy-start.1 = (f32[1024,256]{1,0:T(8,128)S(1)}, f32[1024,256]{1,0:T(8,128)}, u32[]{:S(2)}) copy-start(f32[1024,256]{1,0:T(8,128)} %get-tuple-element.13) | copy-start | bytes 3145732
  128.0 1.6 %copy-start = (f32[1024,256]{1,0:T(8,128)S(1)}, f32[1024,256]{1,0:T(8,128)}, u32[]{:S(2)}) copy-start(f32[1024,256]{1,0:T(8,128)} %get-tuple-element.14) | copy-start | bytes 3145732

commit v3 on v1

v3 whole, which is shorter than its diff:
```python
import jax
import jax.numpy as jnp
from jax import lax
from jax.experimental import pallas as pl
from jax.experimental.pallas import tpu as pltpu
from jax.sharding import PartitionSpec as P

MESH = pl.DeviceIdType.MESH
F32 = jnp.float32
BF16 = jnp.bfloat16


def dot_plain(left, right):
    return jnp.dot(left, right, preferred_element_type=F32)


def dot_last(left, right):
    return lax.dot_general(left, right, (((1,), (1,)), ((), ())), preferred_element_type=F32)


def dot_first(left, right):
    return lax.dot_general(left, right, (((0,), (0,)), ((), ())), preferred_element_type=F32)


SIZES = (64, 64)
STARTS = tuple(sum(SIZES[:r]) for r in range(len(SIZES)))
ROUNDS = len(SIZES)

ORDER = (
    (0, 0, 0), (16,), (1, 0, 0, 3), (2, 0, 0, 1, 0), (1, 0, 0, 1), (2, 0, 0, 0, 0), (2, 0, 0, 1, 3),
    (1, 0, 0, 2), (0, 0, 1), (2, 0, 0, 0, 3), (2, 0, 0, 1, 1), (2, 0, 0, 0, 1), (3, 0, 0, 0), (3, 0, 0, 3),
    (1, 0, 1, 3), (2, 0, 0, 1, 2), (2, 0, 0, 0, 2), (1, 0, 1, 1), (2, 0, 1, 1, 0), (2, 0, 1, 0, 0),
    (2, 0, 1, 1, 3), (3, 0, 0, 1), (1, 0, 1, 2), (0, 1, 0), (3, 0, 0, 2), (2, 0, 1, 0, 3), (2, 0, 1, 1, 1),
    (2, 0, 1, 0, 1), (4, 0, 0), (5, 0, 0, 0, 0), (5, 0, 0, 0, 1), (5, 1, 0, 0, 0), (3, 0, 1, 0), (3, 0, 1, 3),
    (5, 1, 0, 0, 1), (1, 1, 0, 3), (2, 0, 1, 1, 2), (1, 1, 0, 1), (2, 0, 1, 0, 2), (2, 1, 0, 1, 0),
    (5, 0, 0, 1, 0), (2, 1, 0, 0, 0), (5, 0, 0, 1, 1), (2, 1, 0, 1, 3), (1, 1, 0, 2), (0, 1, 1), (3, 0, 1, 1),
    (5, 1, 0, 1, 0), (3, 0, 1, 2), (5, 1, 0, 1, 1), (2, 1, 0, 0, 3), (2, 1, 0, 1, 1), (5, 0, 0, 2, 0),
    (4, 0, 1), (5, 0, 1, 0, 1), (5, 0, 1, 0, 0), (5, 0, 0, 2, 1), (5, 1, 1, 0, 1), (5, 1, 1, 0, 0),
    (2, 1, 0, 0, 1), (3, 1, 0, 3), (3, 1, 0, 0), (5, 1, 0, 2, 0), (2, 1, 0, 1, 2), (1, 1, 1, 3),
    (5, 1, 0, 2, 1), (2, 1, 0, 0, 2), (1, 1, 1, 1), (2, 1, 1, 1, 0), (5, 0, 0, 3, 0), (2, 1, 1, 0, 0),
    (5, 0, 1, 1, 1), (5, 0, 1, 1, 0), (1, 1, 1, 2), (3, 1, 0, 1), (3, 1, 0, 2), (2, 1, 1, 1, 3),
    (2, 1, 1, 0, 3), (5, 1, 1, 1, 0), (2, 1, 1, 1, 1), (4, 1, 0), (5, 2, 0, 0, 1), (2, 1, 1, 0, 1),
    (5, 2, 0, 0, 0), (5, 1, 1, 1, 1), (3, 1, 1, 0), (5, 1, 0, 3, 0), (2, 1, 1, 1, 2), (2, 1, 1, 0, 2),
    (3, 1, 1, 3), (3, 1, 1, 1), (5, 0, 1, 2, 1), (5, 0, 1, 2, 0), (3, 1, 1, 2), (5, 2, 0, 1, 1),
    (5, 1, 1, 2, 0), (4, 1, 1), (5, 2, 1, 0, 1), (5, 2, 1, 0, 0), (5, 1, 1, 2, 1), (5, 2, 0, 1, 0), (6, 0),
    (9, 0, 0, 0, 0), (5, 2, 0, 2, 1), (5, 0, 1, 3, 0), (5, 2, 1, 1, 1), (5, 1, 1, 3, 0), (5, 2, 1, 1, 0),
    (8, 0, 0, 1, 1), (9, 0, 0, 1, 1), (5, 2, 0, 2, 0), (8, 0, 0, 1, 0), (9, 0, 0, 1, 0), (5, 2, 1, 2, 1),
    (8, 0, 0, 2, 1), (9, 0, 0, 2, 1), (6, 1), (9, 0, 1, 0, 0), (5, 2, 1, 2, 0), (5, 2, 0, 3, 0),
    (8, 0, 0, 3, 1), (9, 0, 0, 3, 1), (8, 0, 0, 2, 0), (9, 0, 0, 2, 0), (8, 0, 1, 1, 1), (9, 0, 1, 1, 1),
    (8, 0, 1, 1, 0), (9, 0, 1, 1, 0), (5, 2, 1, 3, 0), (7, 0), (9, 1, 0, 0, 0), (8, 0, 0, 3, 0),
    (9, 0, 0, 3, 0), (8, 0, 1, 2, 1), (9, 0, 1, 2, 1), (8, 0, 1, 2, 0), (9, 0, 1, 2, 0), (7, 1),
    (9, 1, 1, 0, 0), (8, 1, 0, 1, 1), (8, 1, 0, 1, 0), (8, 2, 0, 1, 1), (9, 1, 0, 1, 1), (8, 2, 0, 1, 0),
    (9, 1, 0, 1, 0), (8, 0, 1, 3, 1), (9, 0, 1, 3, 1), (8, 0, 0, 4, 0), (9, 0, 0, 4, 0), (8, 1, 1, 1, 1),
    (8, 0, 1, 3, 0), (9, 0, 1, 3, 0), (10, 0, 0), (11, 0, 0, 0), (11, 0, 0, 2), (11, 0, 0, 1), (11, 0, 0, 3),
    (12, 0, 0, 1, 0), (12, 0, 0, 1, 1), (12, 0, 0, 0, 2), (12, 0, 0, 0, 3), (8, 2, 1, 1, 1), (9, 1, 1, 1, 1),
    (8, 1, 1, 1, 0), (8, 1, 0, 2, 1), (8, 2, 1, 1, 0), (9, 1, 1, 1, 0), (12, 0, 0, 0, 0), (12, 0, 0, 1, 2),
    (12, 0, 0, 0, 1), (12, 0, 0, 1, 3), (8, 2, 0, 2, 1), (9, 1, 0, 2, 1), (8, 1, 0, 2, 0), (8, 1, 1, 2, 1),
    (8, 2, 0, 2, 0), (9, 1, 0, 2, 0), (13, 0, 0, 2), (13, 0, 0, 0), (13, 0, 0, 1), (8, 2, 1, 2, 1),
    (9, 1, 1, 2, 1), (13, 0, 0, 3), (8, 0, 1, 4, 0), (9, 0, 1, 4, 0), (15, 2), (8, 1, 0, 3, 1),
    (8, 1, 1, 2, 0), (10, 0, 1), (11, 0, 1, 0), (11, 0, 1, 2), (11, 0, 1, 1), (11, 0, 1, 3), (12, 0, 1, 1, 1),
    (12, 0, 1, 1, 0), (8, 2, 0, 3, 1), (12, 0, 1, 0, 3), (12, 0, 1, 0, 2), (9, 1, 0, 3, 1), (8, 2, 1, 2, 0),
    (9, 1, 1, 2, 0), (8, 1, 1, 3, 1), (14, 0, 0), (8, 1, 0, 3, 0), (12, 0, 1, 0, 0), (12, 0, 1, 1, 2),
    (8, 2, 1, 3, 1), (9, 1, 1, 3, 1), (8, 2, 0, 3, 0), (9, 1, 0, 3, 0), (12, 0, 1, 1, 3), (8, 1, 1, 3, 0),
    (12, 0, 1, 0, 1), (8, 2, 1, 3, 0), (9, 1, 1, 3, 0), (8, 1, 0, 4, 0), (13, 0, 1, 0), (13, 0, 1, 2),
    (8, 2, 0, 4, 0), (9, 1, 0, 4, 0), (13, 0, 1, 3), (8, 1, 1, 4, 0), (13, 0, 1, 1), (8, 2, 1, 4, 0),
    (9, 1, 1, 4, 0), (10, 1, 0), (11, 1, 0, 1), (11, 1, 0, 3), (11, 1, 0, 0), (11, 1, 0, 2), (12, 1, 0, 0, 2),
    (12, 1, 0, 1, 1), (12, 1, 0, 1, 0), (12, 1, 0, 0, 3), (10, 1, 1), (11, 1, 1, 1), (11, 1, 1, 3),
    (11, 1, 1, 0), (11, 1, 1, 2), (12, 1, 1, 1, 1), (12, 1, 1, 1, 0), (12, 1, 1, 0, 2), (12, 1, 1, 0, 3),
    (14, 0, 1), (12, 1, 0, 1, 3), (12, 1, 0, 0, 1), (12, 1, 0, 1, 2), (12, 1, 0, 0, 0), (12, 1, 1, 1, 3),
    (12, 1, 1, 0, 1), (12, 1, 1, 1, 2), (12, 1, 1, 0, 0), (15, 0), (15, 1), (13, 1, 0, 1), (13, 1, 0, 3),
    (13, 1, 0, 2), (13, 1, 0, 0), (13, 1, 1, 3), (13, 1, 1, 1), (13, 1, 1, 2), (13, 1, 1, 0), (14, 1, 0),
    (14, 1, 1),
)


def kernel(
    tok, wg, wu, wd, grd,
    out_ref, tg_ref, dg_ref, du_ref, dd_ref,
    act, w, rs_send, rs_recv, hall, gu, q, ps, pr, sa, ra, sb, rb, sc, rc,
    dw, outs, local_sem, out_sem, sent, r1, r2, r3, rp, zr, ar, prs, ras, rbs, rcs,
):
    c = lax.axis_index("gx")
    gy = lax.axis_index("gy")
    z = lax.axis_index("gz")
    y, x = gy // 4, gy % 4
    f = x * (1 - c) + y * c
    s = y * (1 - c) + x * c
    fm, sm = 1 + 3 * c, 4 - 3 * c
    sg = 1 - 2 * c
    partner = (1 - c, gy, z)

    def gy_of(f_, s_):
        return ((f_ + 8) % 4) * fm + ((s_ + 8) % 4) * sm

    def at_fs(f_, s_):
        return (c, gy_of(f_, s_), z)

    def mod8(k):
        return (k + 16) % 8

    def at_z(k):
        return (c, gy, mod8(z + k))

    def rows_of(r, block):
        return pl.ds(pl.multiple_of(16 * STARTS[r] + block * SIZES[r], 16), SIZES[r])

    def zrows(r, block):
        return pl.ds(pl.multiple_of(16 * STARTS[r] + block * 2 * SIZES[r], 16), 2 * SIZES[r])

    def round_rows(r):
        return pl.ds(16 * STARTS[r], 16 * SIZES[r])

    def cut(r):
        return pl.ds(STARTS[r], SIZES[r])

    def zcut(r):
        return pl.ds(2 * STARTS[r], 2 * SIZES[r])

    def send(src, dst, family, rs, device):
        pltpu.make_async_remote_copy(
            src_ref=src, dst_ref=dst, send_sem=sent.at[family], recv_sem=rs,
            device_id=device, device_id_type=MESH,
        ).start()

    def recv(dst, rs):
        pltpu.make_async_remote_copy(
            src_ref=dst, dst_ref=dst, send_sem=sent.at[0], recv_sem=rs,
            device_id=partner, device_id_type=MESH,
        ).wait_recv()

    def all_sent(family, ref):
        pltpu.make_async_remote_copy(
            src_ref=ref, dst_ref=ref, send_sem=sent.at[family], recv_sem=local_sem.at[0],
            device_id=partner, device_id_type=MESH,
        ).wait_send()

    barrier = pltpu.get_barrier_semaphore()
    peers = [
        at_fs(f + 1, s), at_fs(f + 2, s), at_fs(f + 3, s), at_fs(f, s + 1), at_fs(f, s + 3),
        at_z(1), at_z(-1), partner,
    ]
    for peer in peers:
        pl.semaphore_signal(barrier, inc=1, device_id=peer, device_id_type=MESH)

    own = (tok, grd)

    def own_rows(a, r):
        return own[a].at[cut(r)]

    locals_ = [
        pltpu.make_async_copy(ref, w.at[k], local_sem.at[k]) for k, ref in enumerate((wg, wu, wd))
    ] + [
        pltpu.make_async_copy(
            own_rows(a, r), act.at[a, c, rows_of(r, gy)], local_sem.at[3 + 2 * r + a]
        )
        for r in range(ROUNDS) for a in range(2)
    ]
    for copy in locals_:
        copy.start()
    pl.semaphore_wait(barrier, len(peers))

    def act_block(a, r, k, t):
        return act.at[a, c, rows_of(r, gy_of(f - k, s + t))]

    def to_partner(a, r, k, t, src=None):
        ref = act_block(a, r, k, t)
        send(
            ref if src is None else src, ref,
            3, rp.at[a, r], partner,
        )

    def gather_own(a, r):
        src = own_rows(a, r)
        ref = act_block(a, r, 0, 0)
        for k in (1, 3, 2):
            send(src, ref, 0, r1.at[a, r, k], at_fs(f + k, s))
        send(src, ref, 1, r2.at[a, r, 0, 0], at_fs(f, s + 1))
        send(src, ref, 1, r2.at[a, r, 1, 0], at_fs(f, s + 3))
        to_partner(a, r, 0, 0, src)

    def gather_row(a, r, k):
        ref = act_block(a, r, k, 0)
        recv(ref, r1.at[a, r, k])
        send(ref, ref, 1, r2.at[a, r, 0, k], at_fs(f, s + 1))
        send(ref, ref, 1, r2.at[a, r, 1, k], at_fs(f, s + 3))
        to_partner(a, r, k, 0)

    def gather_near(a, r, way, k):
        t = (3, 1)[way]
        ref = act_block(a, r, k, t)
        recv(ref, r2.at[a, r, way, k])
        if (way == 0) == (k < 2):
            send(ref, ref, 2, r3.at[a, r, k], at_fs(f, s + 1 + 2 * way))
        to_partner(a, r, k, t)

    def gather_far(a, r, k):
        ref = act_block(a, r, k, 2)
        recv(ref, r3.at[a, r, k])
        to_partner(a, r, k, 2)

    def gather_end(a, r):
        recv(act.at[a, 1 - c, round_rows(r)], rp.at[a, r])
        locals_[3 + 2 * r + a].wait()

    def part(a, r, d):
        rows = zrows(r, d)
        source = 0 if a < 2 else 1
        return dot_plain(act[source, 0, rows, :], w[a, 0:512, :]) + dot_plain(
            act[source, 1, rows, :], w[a, 512:1024, :]
        )

    def sum_recv(a, r, slot):
        recv(rs_recv.at[a, slot, zcut(r)], zr.at[a, r, slot])
        return rs_recv[a, slot, zcut(r), :].astype(F32)

    def sum_step(a, r, j, way):
        slot = 4 * way + j
        to = (-sg, sg)[way]
        value = part(a, r, mod8(z + to * (4 - way - j)))
        if j > 0:
            value = value + sum_recv(a, r, slot - 1)
        rs_send[a, slot, zcut(r), :] = value.astype(BF16)
        send(
            rs_send.at[a, slot, zcut(r)], rs_recv.at[a, slot, zcut(r)],
            4, zr.at[a, r, slot], at_z(to),
        )

    def sum_end(a, r):
        value = part(a, r, z)
        for slot in (3, 6):
            value = value + sum_recv(a, r, slot)
        return value

    def zgather(t, r, j, way):
        slot = 4 * way + j
        to = (-sg, sg)[way]
        ref = hall.at[t, zrows(r, mod8(z - to * j))]
        if j > 0:
            recv(ref, ar.at[t, r, slot - 1])
        if j < 4 - way:
            send(ref, ref, 5, ar.at[t, r, slot], at_z(to))

    def product(o, r, b, half):
        rows = zrows(r, b)
        cols = pl.ds(pl.multiple_of(half * 512, 512), 512)
        if o == 0:
            return dot_last(hall[0, rows, :], w[2, cols, :])
        return dot_last(hall[1, rows, :], w[0, cols, :]) + dot_last(hall[2, rows, :], w[1, cols, :])

    def out_block(o, r, j, way):
        b = mod8(z + (sg, -sg)[way] * j)
        rows = zrows(r, b)
        ps[o, rows, :] = product(o, r, b, 1 - c).astype(BF16)
        send(ps.at[o, rows], pr.at[o, rows], 6, prs.at[o, r], partner)
        q[o, rows, :] = product(o, r, b, c)

    def out_pair(o, r):
        recv(pr.at[o, round_rows(r)], prs.at[o, r])

    done = []

    def put(k, src, dst):
        copy = pltpu.make_async_copy(src, dst, out_sem.at[k])
        copy.start()
        done.append(copy)

    def chip_sum(o, r, k, t):
        rows = rows_of(r, gy_of(f + k, s + t))
        return q[o, rows, :] + pr[o, rows, :].astype(F32)

    def stage_a(o, r, k):
        sa[o, k, cut(r), :] = chip_sum(o, r, k, 2).astype(BF16)
        send(
            sa.at[o, k, cut(r)], ra.at[o, k, cut(r)], 7, ras.at[o, r, k],
            at_fs(f, s + (1 if k < 2 else 3)),
        )

    def stage_b(o, r, way, k):
        t = (1, 3)[way]
        slot = 4 * way + k
        value = chip_sum(o, r, k, t)
        if (way == 0) == (k < 2):
            recv(ra.at[o, k, cut(r)], ras.at[o, r, k])
            value = value + ra[o, k, cut(r), :].astype(F32)
        sb[o, slot, cut(r), :] = value.astype(BF16)
        send(
            sb.at[o, slot, cut(r)], rb.at[o, slot, cut(r)],
            8, rbs.at[o, r, slot], at_fs(f, s + t),
        )

    def stage_c(o, r, k):
        value = chip_sum(o, r, k, 0)
        for slot in (k, 4 + k):
            recv(rb.at[o, slot, cut(r)], rbs.at[o, r, slot])
            value = value + rb[o, slot, cut(r), :].astype(F32)
        if k > 0:
            sc[o, k, cut(r), :] = value.astype(BF16)
            send(
                sc.at[o, k, cut(r)], rc.at[o, k, cut(r)], 9, rcs.at[o, r, k],
                at_fs(f + k, s),
            )
        else:
            q[o, rows_of(r, gy), :] = value

    def stage_d(o, r):
        value = q[o, rows_of(r, gy), :]
        for k in (1, 3, 2):
            recv(rc.at[o, k, cut(r)], rcs.at[o, r, k])
            value = value + rc[o, k, cut(r), :].astype(F32)
        outs[o, cut(r), :] = value.astype(BF16)
        if r == ROUNDS - 1:
            put(o, outs.at[o], (out_ref, tg_ref)[o])

    def weight_grad(k):
        ref, a, t = ((dg_ref, 0, 1), (du_ref, 0, 2), (dd_ref, 1, 0))[k]
        for half in range(2):
            dw[k, half * 512:(half + 1) * 512, :] = dot_first(act[a, half], hall[t])
        put(2 + k, dw.at[k], ref)

    def forward(r):
        gate = sum_end(0, r)
        gu[0, zcut(r), :] = gate
        gated = gate * jax.nn.sigmoid(gate)
        up = sum_end(1, r)
        gu[1, zcut(r), :] = up
        hall[0, zrows(r, z), :] = (gated * up).astype(BF16)
        for way in range(2):
            zgather(0, r, 0, way)

    def backward(r):
        hidden_grad = sum_end(2, r)
        gate = gu[0, zcut(r), :]
        up = gu[1, zcut(r), :]
        sigmoid = jax.nn.sigmoid(gate)
        hall[1, zrows(r, z), :] = (
            hidden_grad * up * sigmoid * (1.0 + gate * (1.0 - sigmoid))
        ).astype(BF16)
        hall[2, zrows(r, z), :] = (hidden_grad * (gate * sigmoid)).astype(BF16)
        for t in (1, 2):
            for way in range(2):
                zgather(t, r, 0, way)

    def weights():
        for copy in locals_[:3]:
            copy.wait()

    phases = (
        gather_own, gather_row, gather_near, gather_far, gather_end, sum_step, forward, backward,
        zgather, out_block, out_pair, stage_a, stage_b, stage_c, stage_d, weight_grad, weights,
    )
    for kind, *rest in ORDER:
        phases[kind](*rest)
    for family, ref in enumerate((
        act.at[0, 0, pl.ds(0, 768)], act.at[0, 0], act.at[0, 0, pl.ds(0, 1024)], act.at[:, 0],
        rs_send, rs_send, ps, sa, sb, sc.at[:, pl.ds(1, 3)],
    )):
        all_sent(family, ref)
    for copy in done:
        copy.wait()


def put_out(*refs):
    sems = refs[10]
    copies = [pltpu.make_async_copy(refs[k], refs[5 + k], sems.at[k]) for k in range(5)]
    for copy in copies:
        copy.start()
    for copy in copies:
        copy.wait()


def per_device(tokens, gate_weight, up_weight, down_weight, out_grad):
    dma = pltpu.SemaphoreType.DMA
    vmem = pltpu.VMEM

    results = pl.pallas_call(
        kernel,
        out_shape=(
            pltpu.VMEM((128, 512), BF16),
            pltpu.VMEM((128, 512), BF16),
            pltpu.VMEM((1024, 256), F32),
            pltpu.VMEM((1024, 256), F32),
            pltpu.VMEM((1024, 256), F32),
        ),
        in_specs=[pl.BlockSpec(memory_space=pltpu.HBM)] * 5,
        out_specs=tuple([pl.BlockSpec(memory_space=pl.ANY)] * 5),
        scratch_shapes=[
            vmem((2, 2, 2048, 512), BF16),
            vmem((3, 1024, 256), BF16),
            vmem((3, 7, 256, 256), BF16),
            vmem((3, 7, 256, 256), BF16),
            vmem((3, 2048, 256), BF16),
            vmem((2, 256, 256), F32),
            vmem((2, 2048, 512), F32),
            vmem((2, 2048, 512), BF16),
            vmem((2, 2048, 512), BF16),
            vmem((2, 4, 128, 512), BF16),
            vmem((2, 4, 128, 512), BF16),
            vmem((2, 8, 128, 512), BF16),
            vmem((2, 8, 128, 512), BF16),
            vmem((2, 4, 128, 512), BF16),
            vmem((2, 4, 128, 512), BF16),
            vmem((3, 1024, 256), F32),
            vmem((2, 128, 512), BF16),
            dma((3 + 2 * ROUNDS,)),
            dma((5,)),
            dma((10,)),
            dma((2, ROUNDS, 4)),
            dma((2, ROUNDS, 2, 4)),
            dma((2, ROUNDS, 4)),
            dma((2, ROUNDS)),
            dma((3, ROUNDS, 7)),
            dma((3, ROUNDS, 7)),
            dma((2, ROUNDS)),
            dma((2, ROUNDS, 4)),
            dma((2, ROUNDS, 8)),
            dma((2, ROUNDS, 4)),
        ],
        compiler_params=pltpu.CompilerParams(
            collective_id=0, has_side_effects=True, vmem_limit_bytes=56 * 1024 * 1024
        ),
        name="slab",
    )(tokens, gate_weight, up_weight, down_weight, out_grad)

    shapes = tuple(jax.ShapeDtypeStruct(value.shape, value.dtype) for value in results)
    return pl.pallas_call(
        put_out,
        out_shape=shapes,
        in_specs=[pl.BlockSpec(memory_space=pl.ANY)] * 5,
        out_specs=tuple([pl.BlockSpec(memory_space=pltpu.HBM)] * 5),
        scratch_shapes=[dma((5,))],
        compiler_params=pltpu.CompilerParams(vmem_limit_bytes=1024 * 1024),
        name="put_out",
    )(*results)


def solution(mesh):
    return jax.shard_map(
        per_device,
        mesh=mesh,
        in_specs=(
            P("gy", ("gz", "gx")),
            P("gz", ("gx", "gy")),
            P("gz", ("gx", "gy")),
            P("gz", ("gx", "gy")),
            P("gy", ("gz", "gx")),
        ),
        out_specs=(
            P("gy", ("gz", "gx")),
            P("gy", ("gz", "gx")),
            P("gz", ("gx", "gy")),
            P("gz", ("gx", "gy")),
            P("gz", ("gx", "gy")),
        ),
        check_vma=False,
    )
```

time: 549 us -> 118 us (0.21)
  waiting for transfers between devices: 497 us -> 0 us
  Pallas kernels: 0 us -> 117 us
  matrix products: 29.4 us -> 0 us
  between operations: 14.3 us -> 0.8 us
    reduce_scatter x6 -> x0, waiting for transfers between devices: 269 us -> none  [the longest x2 154 us: scatter(): return lax.psum_scatter(pair, 'gy', scatter_dimension=0, tiled=True)]
    all_gather x6 -> x0, waiting for transfers between devices: 226 us -> none  [the longest x1 53.9 us: per_device(): x_half = lax.all_gather(tokens, 'gy', axis=0, tiled=True)]
    pallas_call x0 -> x2, Pallas kernels: none -> 117 us  [the longest x1 115 us: per_device(): pl.pallas_call(kernel, out_shape=(pltpu.VMEM((128, 512), BF16), pltpu.VME...]
    dot_general x6 -> x0, matrix products: 29.4 us -> none  [the longest x2 10.5 us: dot_last(): lax.dot_general(left, right, (((1,), (1,)), ((), ())), preferred_element_...]
  transfers between devices with their start and end apart: 12 -> 0, of which waited for: 12 -> 0; matrix products, arithmetic and copies ran while one was open for 6% -> 0% of each run, Pallas kernels for 0% -> 0%
where the time goes in v3:
time: 118 us
  Pallas kernels  117 us (99%)
    pallas_call x1, Pallas kernels, per_device(): pl.pallas_call(kernel, out_shape=(pltpu.VMEM((128, 512), BF16), pltpu.VME...  115 us

profile of v3, /device:TPU:1, one launch (start us, length us, event | category | flops | bytes accessed | tf_op | source)
XLA Modules:
  0.0 117.7 jit_solution(1078382550061260162)
XLA Ops:
  0.6 115.1 %slab.1 = (bf16[128,512]{1,0:T(8,128)(2,1)S(1)}, bf16[128,512]{1,0:T(8,128)(2,1)S(1)}, f32[1024,256]{1,0:T(8,128)S(1)}, f32[1024,256]{1,0:T(8,128)S(1)}, f32[1024,256]{1,0:T(8,128)S(1)}) custom-call(bf16[128,512]{1,0:T(8,128)(2,1)} %tok.1, bf16[1024,256]{1,0:T(8,128)(2,1)} %wg.1, bf16[1024,256]{1,0:T(8,128)(2,1)} %wu.1, bf16[1024,256]{1,0:T(8,128)(2,1)} %wd.1, ...), custom_call_target="tpu_custom_call" | custom-call | tf_op jit(solution)/shard_map/slab/pallas_call | solution.py:375
  115.8 1.8 %put_out.1 = (bf16[128,512]{1,0:T(8,128)(2,1)}, bf16[128,512]{1,0:T(8,128)(2,1)}, f32[1024,256]{1,0:T(8,128)}, f32[1024,256]{1,0:T(8,128)}, f32[1024,256]{1,0:T(8,128)}) custom-call(bf16[128,512]{1,0:T(8,128)(2,1)S(1)} %get-tuple-element.10.refs_0_, bf16[128,512]{1,0:T(8,128)(2,1)S(1)} %get-tuple-element.11.refs_1_, ...), custom_call_target="tpu_custom_call" | custom-call | tf_op jit(solution)/shard_map/put_out/pallas_call | solution.py:425

commit v4 on v3

--- a/solution.py
+++ b/solution.py
@@ -22,54 +22,74 @@
     return lax.dot_general(left, right, (((0,), (0,)), ((), ())), preferred_element_type=F32)
 
 
-SIZES = (64, 64)
+SIZES = (48, 32, 48,)
 STARTS = tuple(sum(SIZES[:r]) for r in range(len(SIZES)))
 ROUNDS = len(SIZES)
 
 ORDER = (
-    (0, 0, 0), (16,), (1, 0, 0, 3), (2, 0, 0, 1, 0), (1, 0, 0, 1), (2, 0, 0, 0, 0), (2, 0, 0, 1, 3),
-    (1, 0, 0, 2), (0, 0, 1), (2, 0, 0, 0, 3), (2, 0, 0, 1, 1), (2, 0, 0, 0, 1), (3, 0, 0, 0), (3, 0, 0, 3),
-    (1, 0, 1, 3), (2, 0, 0, 1, 2), (2, 0, 0, 0, 2), (1, 0, 1, 1), (2, 0, 1, 1, 0), (2, 0, 1, 0, 0),
-    (2, 0, 1, 1, 3), (3, 0, 0, 1), (1, 0, 1, 2), (0, 1, 0), (3, 0, 0, 2), (2, 0, 1, 0, 3), (2, 0, 1, 1, 1),
-    (2, 0, 1, 0, 1), (4, 0, 0), (5, 0, 0, 0, 0), (5, 0, 0, 0, 1), (5, 1, 0, 0, 0), (3, 0, 1, 0), (3, 0, 1, 3),
-    (5, 1, 0, 0, 1), (1, 1, 0, 3), (2, 0, 1, 1, 2), (1, 1, 0, 1), (2, 0, 1, 0, 2), (2, 1, 0, 1, 0),
-    (5, 0, 0, 1, 0), (2, 1, 0, 0, 0), (5, 0, 0, 1, 1), (2, 1, 0, 1, 3), (1, 1, 0, 2), (0, 1, 1), (3, 0, 1, 1),
-    (5, 1, 0, 1, 0), (3, 0, 1, 2), (5, 1, 0, 1, 1), (2, 1, 0, 0, 3), (2, 1, 0, 1, 1), (5, 0, 0, 2, 0),
-    (4, 0, 1), (5, 0, 1, 0, 1), (5, 0, 1, 0, 0), (5, 0, 0, 2, 1), (5, 1, 1, 0, 1), (5, 1, 1, 0, 0),
-    (2, 1, 0, 0, 1), (3, 1, 0, 3), (3, 1, 0, 0), (5, 1, 0, 2, 0), (2, 1, 0, 1, 2), (1, 1, 1, 3),
-    (5, 1, 0, 2, 1), (2, 1, 0, 0, 2), (1, 1, 1, 1), (2, 1, 1, 1, 0), (5, 0, 0, 3, 0), (2, 1, 1, 0, 0),
-    (5, 0, 1, 1, 1), (5, 0, 1, 1, 0), (1, 1, 1, 2), (3, 1, 0, 1), (3, 1, 0, 2), (2, 1, 1, 1, 3),
-    (2, 1, 1, 0, 3), (5, 1, 1, 1, 0), (2, 1, 1, 1, 1), (4, 1, 0), (5, 2, 0, 0, 1), (2, 1, 1, 0, 1),
-    (5, 2, 0, 0, 0), (5, 1, 1, 1, 1), (3, 1, 1, 0), (5, 1, 0, 3, 0), (2, 1, 1, 1, 2), (2, 1, 1, 0, 2),
-    (3, 1, 1, 3), (3, 1, 1, 1), (5, 0, 1, 2, 1), (5, 0, 1, 2, 0), (3, 1, 1, 2), (5, 2, 0, 1, 1),
-    (5, 1, 1, 2, 0), (4, 1, 1), (5, 2, 1, 0, 1), (5, 2, 1, 0, 0), (5, 1, 1, 2, 1), (5, 2, 0, 1, 0), (6, 0),
-    (9, 0, 0, 0, 0), (5, 2, 0, 2, 1), (5, 0, 1, 3, 0), (5, 2, 1, 1, 1), (5, 1, 1, 3, 0), (5, 2, 1, 1, 0),
-    (8, 0, 0, 1, 1), (9, 0, 0, 1, 1), (5, 2, 0, 2, 0), (8, 0, 0, 1, 0), (9, 0, 0, 1, 0), (5, 2, 1, 2, 1),
-    (8, 0, 0, 2, 1), (9, 0, 0, 2, 1), (6, 1), (9, 0, 1, 0, 0), (5, 2, 1, 2, 0), (5, 2, 0, 3, 0),
-    (8, 0, 0, 3, 1), (9, 0, 0, 3, 1), (8, 0, 0, 2, 0), (9, 0, 0, 2, 0), (8, 0, 1, 1, 1), (9, 0, 1, 1, 1),
-    (8, 0, 1, 1, 0), (9, 0, 1, 1, 0), (5, 2, 1, 3, 0), (7, 0), (9, 1, 0, 0, 0), (8, 0, 0, 3, 0),
-    (9, 0, 0, 3, 0), (8, 0, 1, 2, 1), (9, 0, 1, 2, 1), (8, 0, 1, 2, 0), (9, 0, 1, 2, 0), (7, 1),
-    (9, 1, 1, 0, 0), (8, 1, 0, 1, 1), (8, 1, 0, 1, 0), (8, 2, 0, 1, 1), (9, 1, 0, 1, 1), (8, 2, 0, 1, 0),
-    (9, 1, 0, 1, 0), (8, 0, 1, 3, 1), (9, 0, 1, 3, 1), (8, 0, 0, 4, 0), (9, 0, 0, 4, 0), (8, 1, 1, 1, 1),
-    (8, 0, 1, 3, 0), (9, 0, 1, 3, 0), (10, 0, 0), (11, 0, 0, 0), (11, 0, 0, 2), (11, 0, 0, 1), (11, 0, 0, 3),
-    (12, 0, 0, 1, 0), (12, 0, 0, 1, 1), (12, 0, 0, 0, 2), (12, 0, 0, 0, 3), (8, 2, 1, 1, 1), (9, 1, 1, 1, 1),
-    (8, 1, 1, 1, 0), (8, 1, 0, 2, 1), (8, 2, 1, 1, 0), (9, 1, 1, 1, 0), (12, 0, 0, 0, 0), (12, 0, 0, 1, 2),
-    (12, 0, 0, 0, 1), (12, 0, 0, 1, 3), (8, 2, 0, 2, 1), (9, 1, 0, 2, 1), (8, 1, 0, 2, 0), (8, 1, 1, 2, 1),
-    (8, 2, 0, 2, 0), (9, 1, 0, 2, 0), (13, 0, 0, 2), (13, 0, 0, 0), (13, 0, 0, 1), (8, 2, 1, 2, 1),
-    (9, 1, 1, 2, 1), (13, 0, 0, 3), (8, 0, 1, 4, 0), (9, 0, 1, 4, 0), (15, 2), (8, 1, 0, 3, 1),
-    (8, 1, 1, 2, 0), (10, 0, 1), (11, 0, 1, 0), (11, 0, 1, 2), (11, 0, 1, 1), (11, 0, 1, 3), (12, 0, 1, 1, 1),
-    (12, 0, 1, 1, 0), (8, 2, 0, 3, 1), (12, 0, 1, 0, 3), (12, 0, 1, 0, 2), (9, 1, 0, 3, 1), (8, 2, 1, 2, 0),
-    (9, 1, 1, 2, 0), (8, 1, 1, 3, 1), (14, 0, 0), (8, 1, 0, 3, 0), (12, 0, 1, 0, 0), (12, 0, 1, 1, 2),
-    (8, 2, 1, 3, 1), (9, 1, 1, 3, 1), (8, 2, 0, 3, 0), (9, 1, 0, 3, 0), (12, 0, 1, 1, 3), (8, 1, 1, 3, 0),
-    (12, 0, 1, 0, 1), (8, 2, 1, 3, 0), (9, 1, 1, 3, 0), (8, 1, 0, 4, 0), (13, 0, 1, 0), (13, 0, 1, 2),
-    (8, 2, 0, 4, 0), (9, 1, 0, 4, 0), (13, 0, 1, 3), (8, 1, 1, 4, 0), (13, 0, 1, 1), (8, 2, 1, 4, 0),
-    (9, 1, 1, 4, 0), (10, 1, 0), (11, 1, 0, 1), (11, 1, 0, 3), (11, 1, 0, 0), (11, 1, 0, 2), (12, 1, 0, 0, 2),
-    (12, 1, 0, 1, 1), (12, 1, 0, 1, 0), (12, 1, 0, 0, 3), (10, 1, 1), (11, 1, 1, 1), (11, 1, 1, 3),
-    (11, 1, 1, 0), (11, 1, 1, 2), (12, 1, 1, 1, 1), (12, 1, 1, 1, 0), (12, 1, 1, 0, 2), (12, 1, 1, 0, 3),
-    (14, 0, 1), (12, 1, 0, 1, 3), (12, 1, 0, 0, 1), (12, 1, 0, 1, 2), (12, 1, 0, 0, 0), (12, 1, 1, 1, 3),
-    (12, 1, 1, 0, 1), (12, 1, 1, 1, 2), (12, 1, 1, 0, 0), (15, 0), (15, 1), (13, 1, 0, 1), (13, 1, 0, 3),
-    (13, 1, 0, 2), (13, 1, 0, 0), (13, 1, 1, 3), (13, 1, 1, 1), (13, 1, 1, 2), (13, 1, 1, 0), (14, 1, 0),
-    (14, 1, 1),
+    (0, 0, 0), (16,), (2, 0, 0, 1, 0), (1, 0, 0, 3), (1, 0, 0, 1), (2, 0, 0, 0, 0), (1, 0, 0, 2), (0, 0, 1),
+    (2, 0, 0, 1, 3), (2, 0, 0, 0, 3), (2, 0, 0, 1, 1), (2, 0, 0, 0, 1), (3, 0, 0, 0), (1, 0, 1, 3),
+    (2, 0, 0, 1, 2), (1, 0, 1, 1), (2, 0, 0, 0, 2), (2, 0, 1, 1, 0), (2, 0, 1, 0, 0), (3, 0, 0, 3),
+    (1, 0, 1, 2), (0, 0, 2), (3, 0, 0, 1), (2, 0, 1, 1, 3), (2, 0, 1, 0, 3), (2, 0, 1, 0, 1), (3, 0, 0, 2),
+    (3, 0, 1, 0), (2, 0, 1, 1, 1), (4, 0, 0), (5, 0, 0, 0, 0), (5, 1, 0, 0, 0), (2, 0, 1, 1, 2),
+    (5, 0, 0, 0, 1), (2, 0, 1, 0, 2), (5, 1, 0, 0, 1), (1, 0, 2, 3), (2, 0, 2, 1, 0), (1, 0, 2, 1),
+    (3, 0, 1, 3), (2, 0, 2, 0, 0), (3, 0, 1, 1), (1, 0, 2, 2), (0, 1, 0), (5, 0, 0, 1, 0), (3, 0, 1, 2),
+    (5, 1, 0, 1, 0), (5, 0, 0, 1, 1), (2, 0, 2, 0, 3), (5, 1, 0, 1, 1), (2, 0, 2, 1, 3), (4, 0, 1),
+    (5, 0, 1, 0, 1), (2, 0, 2, 0, 1), (2, 0, 2, 1, 1), (5, 1, 1, 0, 0), (5, 0, 1, 0, 0), (5, 1, 1, 0, 1),
+    (3, 0, 2, 0), (5, 0, 0, 2, 0), (2, 0, 2, 1, 2), (1, 1, 0, 3), (5, 1, 0, 2, 0), (1, 1, 0, 1),
+    (2, 1, 0, 1, 0), (2, 0, 2, 0, 2), (5, 0, 0, 2, 1), (2, 1, 0, 0, 0), (3, 0, 2, 3), (5, 1, 0, 2, 1),
+    (5, 1, 1, 1, 0), (5, 0, 1, 1, 1), (3, 0, 2, 1), (1, 1, 0, 2), (0, 1, 1), (5, 0, 1, 1, 0), (5, 1, 1, 1, 1),
+    (3, 0, 2, 2), (5, 0, 0, 3, 0), (2, 1, 0, 0, 3), (2, 1, 0, 1, 3), (2, 1, 0, 0, 1), (5, 1, 0, 3, 0),
+    (4, 0, 2), (2, 1, 0, 1, 1), (5, 0, 2, 0, 1), (3, 1, 0, 0), (5, 0, 2, 0, 0), (5, 1, 1, 2, 0),
+    (5, 1, 2, 0, 0), (5, 1, 2, 0, 1), (5, 0, 1, 2, 0), (1, 1, 1, 3), (5, 0, 1, 2, 1), (2, 1, 0, 1, 2),
+    (1, 1, 1, 1), (2, 1, 0, 0, 2), (2, 1, 1, 1, 0), (5, 1, 1, 2, 1), (2, 1, 1, 0, 0), (3, 1, 0, 3), (6, 0),
+    (3, 1, 0, 1), (1, 1, 1, 2), (0, 1, 2), (9, 0, 0, 0, 0), (5, 0, 2, 1, 0), (5, 0, 2, 1, 1), (5, 1, 1, 3, 0),
+    (2, 1, 1, 1, 3), (2, 1, 1, 0, 3), (5, 1, 2, 1, 1), (2, 1, 1, 0, 1), (3, 1, 0, 2), (3, 1, 1, 0),
+    (5, 1, 2, 1, 0), (2, 1, 1, 1, 1), (5, 0, 1, 3, 0), (4, 1, 0), (5, 2, 0, 0, 1), (5, 2, 0, 0, 0),
+    (8, 0, 0, 1, 1), (9, 0, 0, 1, 1), (2, 1, 1, 1, 2), (2, 1, 1, 0, 2), (8, 0, 0, 1, 0), (9, 0, 0, 1, 0),
+    (1, 1, 2, 3), (2, 1, 2, 1, 0), (5, 0, 2, 2, 1), (1, 1, 2, 1), (3, 1, 1, 3), (5, 0, 2, 2, 0),
+    (2, 1, 2, 0, 0), (3, 1, 1, 1), (5, 1, 2, 2, 1), (1, 1, 2, 2), (5, 1, 2, 2, 0), (5, 2, 0, 1, 1), (6, 1),
+    (3, 1, 1, 2), (8, 0, 0, 2, 1), (9, 0, 0, 2, 1), (2, 1, 2, 0, 3), (2, 1, 2, 1, 3), (5, 2, 0, 1, 0),
+    (9, 0, 1, 0, 0), (2, 1, 2, 0, 1), (2, 1, 2, 1, 1), (4, 1, 1), (3, 1, 2, 0), (5, 2, 1, 0, 1),
+    (2, 1, 2, 1, 2), (8, 0, 0, 2, 0), (9, 0, 0, 2, 0), (2, 1, 2, 0, 2), (5, 2, 1, 0, 0), (5, 0, 2, 3, 0),
+    (5, 2, 0, 2, 1), (5, 1, 2, 3, 0), (8, 0, 1, 1, 1), (9, 0, 1, 1, 1), (3, 1, 2, 3), (8, 0, 1, 1, 0),
+    (9, 0, 1, 1, 0), (3, 1, 2, 1), (8, 0, 0, 3, 1), (9, 0, 0, 3, 1), (3, 1, 2, 2), (5, 2, 0, 2, 0),
+    (5, 2, 1, 1, 1), (8, 0, 0, 3, 0), (9, 0, 0, 3, 0), (4, 1, 2), (5, 2, 2, 0, 0), (5, 2, 1, 1, 0),
+    (5, 2, 2, 0, 1), (8, 0, 1, 2, 1), (9, 0, 1, 2, 1), (6, 2), (5, 2, 1, 2, 1), (8, 0, 1, 2, 0),
+    (9, 0, 1, 2, 0), (5, 2, 0, 3, 0), (8, 0, 0, 4, 0), (9, 0, 0, 4, 0), (9, 0, 2, 0, 0), (5, 2, 2, 1, 1),
+    (5, 2, 2, 1, 0), (8, 0, 1, 3, 1), (9, 0, 1, 3, 1), (10, 0, 0), (11, 0, 0, 0), (11, 0, 0, 2), (11, 0, 0, 1),
+    (11, 0, 0, 3), (12, 0, 0, 1, 1), (12, 0, 0, 1, 0), (12, 0, 0, 0, 2), (5, 2, 1, 2, 0), (12, 0, 0, 0, 3),
+    (8, 0, 2, 1, 1), (8, 0, 2, 1, 0), (9, 0, 2, 1, 1), (9, 0, 2, 1, 0), (8, 0, 1, 3, 0), (9, 0, 1, 3, 0),
+    (7, 0), (9, 1, 0, 0, 0), (12, 0, 0, 0, 0), (12, 0, 0, 1, 2), (5, 2, 2, 2, 0), (5, 2, 1, 3, 0),
+    (12, 0, 0, 0, 1), (12, 0, 0, 1, 3), (5, 2, 2, 2, 1), (8, 0, 2, 2, 1), (8, 0, 2, 2, 0), (9, 0, 2, 2, 1),
+    (8, 0, 1, 4, 0), (9, 0, 1, 4, 0), (9, 0, 2, 2, 0), (8, 1, 0, 1, 0), (8, 1, 0, 1, 1), (10, 0, 1),
+    (11, 0, 1, 3), (11, 0, 1, 0), (11, 0, 1, 2), (11, 0, 1, 1), (12, 0, 1, 1, 0), (13, 0, 0, 0), (13, 0, 0, 2),
+    (12, 0, 1, 0, 3), (12, 0, 1, 0, 2), (8, 2, 0, 1, 0), (8, 2, 0, 1, 1), (9, 1, 0, 1, 0), (13, 0, 0, 1),
+    (9, 1, 0, 1, 1), (13, 0, 0, 3), (5, 2, 2, 3, 0), (7, 1), (9, 1, 1, 0, 0), (12, 0, 1, 0, 0),
+    (12, 0, 1, 1, 3), (12, 0, 1, 1, 1), (12, 0, 1, 1, 2), (8, 0, 2, 3, 1), (8, 1, 0, 2, 1), (9, 0, 2, 3, 1),
+    (12, 0, 1, 0, 1), (8, 0, 2, 3, 0), (9, 0, 2, 3, 0), (8, 1, 0, 2, 0), (8, 2, 0, 2, 1), (9, 1, 0, 2, 1),
+    (8, 2, 0, 2, 0), (9, 1, 0, 2, 0), (8, 1, 1, 1, 1), (7, 2), (14, 0, 0), (8, 2, 1, 1, 1), (8, 1, 1, 1, 0),
+    (13, 0, 1, 3), (9, 1, 1, 1, 1), (13, 0, 1, 0), (8, 2, 1, 1, 0), (13, 0, 1, 1), (13, 0, 1, 2),
+    (8, 1, 0, 3, 1), (9, 1, 1, 1, 0), (9, 1, 2, 0, 0), (8, 2, 0, 3, 1), (9, 1, 0, 3, 1), (8, 0, 2, 4, 0),
+    (8, 1, 1, 2, 1), (9, 0, 2, 4, 0), (8, 1, 0, 3, 0), (15, 2), (8, 2, 0, 3, 0), (9, 1, 0, 3, 0),
+    (8, 1, 2, 1, 0), (8, 1, 2, 1, 1), (10, 0, 2), (11, 0, 2, 2), (11, 0, 2, 1), (11, 0, 2, 3), (8, 2, 1, 2, 1),
+    (9, 1, 1, 2, 1), (14, 0, 1), (8, 1, 1, 3, 1), (11, 0, 2, 0), (12, 0, 2, 1, 0), (12, 0, 2, 0, 3),
+    (8, 1, 1, 2, 0), (12, 0, 2, 0, 2), (8, 2, 2, 1, 0), (9, 1, 2, 1, 0), (8, 2, 1, 2, 0), (9, 1, 1, 2, 0),
+    (8, 1, 0, 4, 0), (12, 0, 2, 1, 1), (8, 2, 2, 1, 1), (9, 1, 2, 1, 1), (8, 2, 0, 4, 0), (9, 1, 0, 4, 0),
+    (8, 1, 2, 2, 1), (12, 0, 2, 0, 1), (12, 0, 2, 1, 2), (8, 1, 2, 2, 0), (8, 2, 1, 3, 1), (9, 1, 1, 3, 1),
+    (8, 1, 1, 3, 0), (12, 0, 2, 1, 3), (12, 0, 2, 0, 0), (8, 2, 2, 2, 0), (9, 1, 2, 2, 0), (10, 1, 0),
+    (11, 1, 0, 1), (11, 1, 0, 3), (11, 1, 0, 0), (11, 1, 0, 2), (12, 1, 0, 1, 0), (12, 1, 0, 0, 2),
+    (12, 1, 0, 0, 3), (12, 1, 0, 1, 1), (8, 2, 1, 3, 0), (9, 1, 1, 3, 0), (8, 2, 2, 2, 1), (9, 1, 2, 2, 1),
+    (8, 1, 2, 3, 1), (8, 1, 2, 3, 0), (13, 0, 2, 2), (13, 0, 2, 1), (8, 1, 1, 4, 0), (8, 2, 2, 3, 0),
+    (9, 1, 2, 3, 0), (13, 0, 2, 3), (13, 0, 2, 0), (8, 2, 1, 4, 0), (9, 1, 1, 4, 0), (12, 1, 0, 1, 3),
+    (12, 1, 0, 0, 1), (12, 1, 0, 0, 0), (12, 1, 0, 1, 2), (8, 2, 2, 3, 1), (9, 1, 2, 3, 1), (8, 1, 2, 4, 0),
+    (10, 1, 1), (11, 1, 1, 3), (11, 1, 1, 0), (11, 1, 1, 2), (11, 1, 1, 1), (12, 1, 1, 1, 0), (12, 1, 1, 1, 1),
+    (12, 1, 1, 0, 2), (12, 1, 1, 0, 3), (8, 2, 2, 4, 0), (9, 1, 2, 4, 0), (13, 1, 0, 3), (10, 1, 2),
+    (11, 1, 2, 2), (11, 1, 2, 0), (11, 1, 2, 1), (11, 1, 2, 3), (13, 1, 0, 1), (13, 1, 0, 2), (12, 1, 2, 0, 2),
+    (12, 1, 2, 1, 0), (12, 1, 2, 1, 1), (12, 1, 2, 0, 3), (12, 1, 1, 1, 3), (14, 0, 2), (13, 1, 0, 0),
+    (12, 1, 1, 1, 2), (12, 1, 1, 0, 0), (12, 1, 1, 0, 1), (12, 1, 2, 1, 2), (12, 1, 2, 0, 0), (15, 1),
+    (12, 1, 2, 0, 1), (12, 1, 2, 1, 3), (15, 0), (13, 1, 1, 2), (13, 1, 1, 3), (14, 1, 0), (13, 1, 2, 2),
+    (13, 1, 1, 0), (13, 1, 1, 1), (13, 1, 2, 0), (13, 1, 2, 1), (13, 1, 2, 3), (14, 1, 1), (14, 1, 2),
 )
 
 
@@ -155,7 +175,7 @@
         )
         for r in range(ROUNDS) for a in range(2)
     ]
-    for copy in locals_:
+    for copy in locals_[3:] + locals_[:3]:
         copy.start()
     pl.semaphore_wait(barrier, len(peers))
 
@@ -170,17 +190,17 @@
         )
 
     def gather_own(a, r):
-        src = own_rows(a, r)
-        ref = act_block(a, r, 0, 0)
+        ref = src = act_block(a, r, 0, 0)
+        locals_[3 + 2 * r + a].wait()
         for k in (1, 3, 2):
-            send(src, ref, 0, r1.at[a, r, k], at_fs(f + k, s))
+            send(src, ref, 0, r1.at[a, r, k - 1], at_fs(f + k, s))
         send(src, ref, 1, r2.at[a, r, 0, 0], at_fs(f, s + 1))
         send(src, ref, 1, r2.at[a, r, 1, 0], at_fs(f, s + 3))
         to_partner(a, r, 0, 0, src)
 
     def gather_row(a, r, k):
         ref = act_block(a, r, k, 0)
-        recv(ref, r1.at[a, r, k])
+        recv(ref, r1.at[a, r, k - 1])
         send(ref, ref, 1, r2.at[a, r, 0, k], at_fs(f, s + 1))
         send(ref, ref, 1, r2.at[a, r, 1, k], at_fs(f, s + 3))
         to_partner(a, r, k, 0)
@@ -200,7 +220,6 @@
 
     def gather_end(a, r):
         recv(act.at[a, 1 - c, round_rows(r)], rp.at[a, r])
-        locals_[3 + 2 * r + a].wait()
 
     def part(a, r, d):
         rows = zrows(r, d)
@@ -277,26 +296,25 @@
 
     def stage_b(o, r, way, k):
         t = (1, 3)[way]
-        slot = 4 * way + k
         value = chip_sum(o, r, k, t)
         if (way == 0) == (k < 2):
             recv(ra.at[o, k, cut(r)], ras.at[o, r, k])
             value = value + ra[o, k, cut(r), :].astype(F32)
-        sb[o, slot, cut(r), :] = value.astype(BF16)
+        sb[o, k, way, cut(r), :] = value.astype(BF16)
         send(
-            sb.at[o, slot, cut(r)], rb.at[o, slot, cut(r)],
-            8, rbs.at[o, r, slot], at_fs(f, s + t),
+            sb.at[o, k, way, cut(r)], rb.at[o, k, way, cut(r)],
+            8, rbs.at[o, r, k], at_fs(f, s + t),
         )
 
     def stage_c(o, r, k):
         value = chip_sum(o, r, k, 0)
-        for slot in (k, 4 + k):
-            recv(rb.at[o, slot, cut(r)], rbs.at[o, r, slot])
-            value = value + rb[o, slot, cut(r), :].astype(F32)
+        recv(rb.at[o, k, :, cut(r)], rbs.at[o, r, k])
+        for way in range(2):
+            value = value + rb[o, k, way, cut(r), :].astype(F32)
         if k > 0:
             sc[o, k, cut(r), :] = value.astype(BF16)
             send(
-                sc.at[o, k, cut(r)], rc.at[o, k, cut(r)], 9, rcs.at[o, r, k],
+                sc.at[o, k, cut(r)], rc.at[o, k, cut(r)], 9, rcs.at[o, r],
                 at_fs(f + k, s),
             )
         else:
@@ -304,8 +322,8 @@
 
     def stage_d(o, r):
         value = q[o, rows_of(r, gy), :]
+        recv(rc.at[o, pl.ds(1, 3), cut(r)], rcs.at[o, r])
         for k in (1, 3, 2):
-            recv(rc.at[o, k, cut(r)], rcs.at[o, r, k])
             value = value + rc[o, k, cut(r), :].astype(F32)
         outs[o, cut(r), :] = value.astype(BF16)
         if r == ROUNDS - 1:
@@ -361,7 +379,13 @@
 
 def put_out(*refs):
     sems = refs[10]
-    copies = [pltpu.make_async_copy(refs[k], refs[5 + k], sems.at[k]) for k in range(5)]
+    copies = [pltpu.make_async_copy(refs[k], refs[5 + k], sems.at[k]) for k in range(2)] + [
+        pltpu.make_async_copy(
+            refs[k].at[pl.ds(256 * n, 256)], refs[5 + k].at[pl.ds(256 * n, 256)],
+            sems.at[2 + 4 * (k - 2) + n],
+        )
+        for k in range(2, 5) for n in range(4)
+    ]
     for copy in copies:
         copy.start()
     for copy in copies:
@@ -395,8 +419,8 @@
             vmem((2, 2048, 512), BF16),
             vmem((2, 4, 128, 512), BF16),
             vmem((2, 4, 128, 512), BF16),
-            vmem((2, 8, 128, 512), BF16),
-            vmem((2, 8, 128, 512), BF16),
+            vmem((2, 4, 2, 128, 512), BF16),
+            vmem((2, 4, 2, 128, 512), BF16),
             vmem((2, 4, 128, 512), BF16),
             vmem((2, 4, 128, 512), BF16),
             vmem((3, 1024, 256), F32),
@@ -404,7 +428,7 @@
             dma((3 + 2 * ROUNDS,)),
             dma((5,)),
             dma((10,)),
-            dma((2, ROUNDS, 4)),
+            dma((2, ROUNDS, 3)),
             dma((2, ROUNDS, 2, 4)),
             dma((2, ROUNDS, 4)),
             dma((2, ROUNDS)),
@@ -412,8 +436,8 @@
             dma((3, ROUNDS, 7)),
             dma((2, ROUNDS)),
             dma((2, ROUNDS, 4)),
-            dma((2, ROUNDS, 8)),
             dma((2, ROUNDS, 4)),
+            dma((2, ROUNDS)),
         ],
         compiler_params=pltpu.CompilerParams(
             collective_id=0, has_side_effects=True, vmem_limit_bytes=56 * 1024 * 1024
@@ -427,7 +451,7 @@
         out_shape=shapes,
         in_specs=[pl.BlockSpec(memory_space=pl.ANY)] * 5,
         out_specs=tuple([pl.BlockSpec(memory_space=pltpu.HBM)] * 5),
-        scratch_shapes=[dma((5,))],
+        scratch_shapes=[dma((14,))],
         compiler_params=pltpu.CompilerParams(vmem_limit_bytes=1024 * 1024),
         name="put_out",
     )(*results)

time: 118 us -> 111 us (0.941)
  Pallas kernels: 117 us -> 109 us
    pallas_call x1, Pallas kernels: 115 us -> 107 us  [per_device(): pl.pallas_call(kernel, out_shape=(pltpu.VMEM((128, 512), BF16), pltpu.VME...]
where the time goes in v4:
time: 111 us; the launch traced here: 110 us
  Pallas kernels  109 us (98%)
    pallas_call x1, Pallas kernels, per_device(): pl.pallas_call(kernel, out_shape=(pltpu.VMEM((128, 512), BF16), pltpu.VME...  107 us

profile of v4, /device:TPU:1, one launch (start us, length us, event | category | flops | bytes accessed | tf_op | source)
XLA Modules:
  0.0 109.6 jit_solution(2062271771709798302)
XLA Ops:
  0.6 107.0 %slab.1 = (bf16[128,512]{1,0:T(8,128)(2,1)S(1)}, bf16[128,512]{1,0:T(8,128)(2,1)S(1)}, f32[1024,256]{1,0:T(8,128)S(1)}, f32[1024,256]{1,0:T(8,128)S(1)}, f32[1024,256]{1,0:T(8,128)S(1)}) custom-call(bf16[128,512]{1,0:T(8,128)(2,1)} %tok.1, bf16[1024,256]{1,0:T(8,128)(2,1)} %wg.1, bf16[1024,256]{1,0:T(8,128)(2,1)} %wu.1, bf16[1024,256]{1,0:T(8,128)(2,1)} %wd.1, ...), custom_call_target="tpu_custom_call" | custom-call | tf_op jit(solution)/shard_map/slab/pallas_call | solution.py:399
  107.6 1.9 %put_out.1 = (bf16[128,512]{1,0:T(8,128)(2,1)}, bf16[128,512]{1,0:T(8,128)(2,1)}, f32[1024,256]{1,0:T(8,128)}, f32[1024,256]{1,0:T(8,128)}, f32[1024,256]{1,0:T(8,128)}) custom-call(bf16[128,512]{1,0:T(8,128)(2,1)S(1)} %get-tuple-element.10.refs_0_, bf16[128,512]{1,0:T(8,128)(2,1)S(1)} %get-tuple-element.11.refs_1_, ...), custom_call_target="tpu_custom_call" | custom-call | tf_op jit(solution)/shard_map/put_out/pallas_call | solution.py:449

commit v5 on v4

--- a/solution.py
+++ b/solution.py
@@ -27,69 +27,69 @@
 ROUNDS = len(SIZES)
 
 ORDER = (
-    (0, 0, 0), (16,), (2, 0, 0, 1, 0), (1, 0, 0, 3), (1, 0, 0, 1), (2, 0, 0, 0, 0), (1, 0, 0, 2), (0, 0, 1),
-    (2, 0, 0, 1, 3), (2, 0, 0, 0, 3), (2, 0, 0, 1, 1), (2, 0, 0, 0, 1), (3, 0, 0, 0), (1, 0, 1, 3),
+    (0, 0, 0), (16,), (1, 0, 0, 3), (2, 0, 0, 1, 0), (1, 0, 0, 1), (2, 0, 0, 0, 0), (1, 0, 0, 2), (0, 0, 1),
+    (2, 0, 0, 0, 3), (2, 0, 0, 1, 3), (2, 0, 0, 1, 1), (2, 0, 0, 0, 1), (3, 0, 0, 0), (1, 0, 1, 3),
     (2, 0, 0, 1, 2), (1, 0, 1, 1), (2, 0, 0, 0, 2), (2, 0, 1, 1, 0), (2, 0, 1, 0, 0), (3, 0, 0, 3),
     (1, 0, 1, 2), (0, 0, 2), (3, 0, 0, 1), (2, 0, 1, 1, 3), (2, 0, 1, 0, 3), (2, 0, 1, 0, 1), (3, 0, 0, 2),
     (3, 0, 1, 0), (2, 0, 1, 1, 1), (4, 0, 0), (5, 0, 0, 0, 0), (5, 1, 0, 0, 0), (2, 0, 1, 1, 2),
-    (5, 0, 0, 0, 1), (2, 0, 1, 0, 2), (5, 1, 0, 0, 1), (1, 0, 2, 3), (2, 0, 2, 1, 0), (1, 0, 2, 1),
+    (5, 1, 0, 0, 1), (2, 0, 1, 0, 2), (5, 0, 0, 0, 1), (1, 0, 2, 3), (2, 0, 2, 1, 0), (1, 0, 2, 1),
     (3, 0, 1, 3), (2, 0, 2, 0, 0), (3, 0, 1, 1), (1, 0, 2, 2), (0, 1, 0), (5, 0, 0, 1, 0), (3, 0, 1, 2),
-    (5, 1, 0, 1, 0), (5, 0, 0, 1, 1), (2, 0, 2, 0, 3), (5, 1, 0, 1, 1), (2, 0, 2, 1, 3), (4, 0, 1),
-    (5, 0, 1, 0, 1), (2, 0, 2, 0, 1), (2, 0, 2, 1, 1), (5, 1, 1, 0, 0), (5, 0, 1, 0, 0), (5, 1, 1, 0, 1),
-    (3, 0, 2, 0), (5, 0, 0, 2, 0), (2, 0, 2, 1, 2), (1, 1, 0, 3), (5, 1, 0, 2, 0), (1, 1, 0, 1),
-    (2, 1, 0, 1, 0), (2, 0, 2, 0, 2), (5, 0, 0, 2, 1), (2, 1, 0, 0, 0), (3, 0, 2, 3), (5, 1, 0, 2, 1),
-    (5, 1, 1, 1, 0), (5, 0, 1, 1, 1), (3, 0, 2, 1), (1, 1, 0, 2), (0, 1, 1), (5, 0, 1, 1, 0), (5, 1, 1, 1, 1),
+    (5, 1, 0, 1, 0), (5, 1, 0, 1, 1), (2, 0, 2, 1, 3), (2, 0, 2, 0, 3), (5, 0, 0, 1, 1), (4, 0, 1),
+    (5, 1, 1, 0, 1), (2, 0, 2, 0, 1), (2, 0, 2, 1, 1), (5, 1, 1, 0, 0), (5, 0, 1, 0, 1), (3, 0, 2, 0),
+    (5, 0, 1, 0, 0), (5, 0, 0, 2, 0), (2, 0, 2, 1, 2), (1, 1, 0, 3), (5, 1, 0, 2, 0), (2, 1, 0, 1, 0),
+    (2, 0, 2, 0, 2), (1, 1, 0, 1), (5, 1, 0, 2, 1), (3, 0, 2, 3), (2, 1, 0, 0, 0), (5, 0, 0, 2, 1),
+    (5, 1, 1, 1, 0), (5, 1, 1, 1, 1), (3, 0, 2, 1), (1, 1, 0, 2), (0, 1, 1), (5, 0, 1, 1, 0), (5, 0, 1, 1, 1),
     (3, 0, 2, 2), (5, 0, 0, 3, 0), (2, 1, 0, 0, 3), (2, 1, 0, 1, 3), (2, 1, 0, 0, 1), (5, 1, 0, 3, 0),
-    (4, 0, 2), (2, 1, 0, 1, 1), (5, 0, 2, 0, 1), (3, 1, 0, 0), (5, 0, 2, 0, 0), (5, 1, 1, 2, 0),
-    (5, 1, 2, 0, 0), (5, 1, 2, 0, 1), (5, 0, 1, 2, 0), (1, 1, 1, 3), (5, 0, 1, 2, 1), (2, 1, 0, 1, 2),
-    (1, 1, 1, 1), (2, 1, 0, 0, 2), (2, 1, 1, 1, 0), (5, 1, 1, 2, 1), (2, 1, 1, 0, 0), (3, 1, 0, 3), (6, 0),
-    (3, 1, 0, 1), (1, 1, 1, 2), (0, 1, 2), (9, 0, 0, 0, 0), (5, 0, 2, 1, 0), (5, 0, 2, 1, 1), (5, 1, 1, 3, 0),
-    (2, 1, 1, 1, 3), (2, 1, 1, 0, 3), (5, 1, 2, 1, 1), (2, 1, 1, 0, 1), (3, 1, 0, 2), (3, 1, 1, 0),
-    (5, 1, 2, 1, 0), (2, 1, 1, 1, 1), (5, 0, 1, 3, 0), (4, 1, 0), (5, 2, 0, 0, 1), (5, 2, 0, 0, 0),
-    (8, 0, 0, 1, 1), (9, 0, 0, 1, 1), (2, 1, 1, 1, 2), (2, 1, 1, 0, 2), (8, 0, 0, 1, 0), (9, 0, 0, 1, 0),
-    (1, 1, 2, 3), (2, 1, 2, 1, 0), (5, 0, 2, 2, 1), (1, 1, 2, 1), (3, 1, 1, 3), (5, 0, 2, 2, 0),
-    (2, 1, 2, 0, 0), (3, 1, 1, 1), (5, 1, 2, 2, 1), (1, 1, 2, 2), (5, 1, 2, 2, 0), (5, 2, 0, 1, 1), (6, 1),
-    (3, 1, 1, 2), (8, 0, 0, 2, 1), (9, 0, 0, 2, 1), (2, 1, 2, 0, 3), (2, 1, 2, 1, 3), (5, 2, 0, 1, 0),
-    (9, 0, 1, 0, 0), (2, 1, 2, 0, 1), (2, 1, 2, 1, 1), (4, 1, 1), (3, 1, 2, 0), (5, 2, 1, 0, 1),
-    (2, 1, 2, 1, 2), (8, 0, 0, 2, 0), (9, 0, 0, 2, 0), (2, 1, 2, 0, 2), (5, 2, 1, 0, 0), (5, 0, 2, 3, 0),
-    (5, 2, 0, 2, 1), (5, 1, 2, 3, 0), (8, 0, 1, 1, 1), (9, 0, 1, 1, 1), (3, 1, 2, 3), (8, 0, 1, 1, 0),
-    (9, 0, 1, 1, 0), (3, 1, 2, 1), (8, 0, 0, 3, 1), (9, 0, 0, 3, 1), (3, 1, 2, 2), (5, 2, 0, 2, 0),
-    (5, 2, 1, 1, 1), (8, 0, 0, 3, 0), (9, 0, 0, 3, 0), (4, 1, 2), (5, 2, 2, 0, 0), (5, 2, 1, 1, 0),
-    (5, 2, 2, 0, 1), (8, 0, 1, 2, 1), (9, 0, 1, 2, 1), (6, 2), (5, 2, 1, 2, 1), (8, 0, 1, 2, 0),
-    (9, 0, 1, 2, 0), (5, 2, 0, 3, 0), (8, 0, 0, 4, 0), (9, 0, 0, 4, 0), (9, 0, 2, 0, 0), (5, 2, 2, 1, 1),
-    (5, 2, 2, 1, 0), (8, 0, 1, 3, 1), (9, 0, 1, 3, 1), (10, 0, 0), (11, 0, 0, 0), (11, 0, 0, 2), (11, 0, 0, 1),
-    (11, 0, 0, 3), (12, 0, 0, 1, 1), (12, 0, 0, 1, 0), (12, 0, 0, 0, 2), (5, 2, 1, 2, 0), (12, 0, 0, 0, 3),
-    (8, 0, 2, 1, 1), (8, 0, 2, 1, 0), (9, 0, 2, 1, 1), (9, 0, 2, 1, 0), (8, 0, 1, 3, 0), (9, 0, 1, 3, 0),
-    (7, 0), (9, 1, 0, 0, 0), (12, 0, 0, 0, 0), (12, 0, 0, 1, 2), (5, 2, 2, 2, 0), (5, 2, 1, 3, 0),
-    (12, 0, 0, 0, 1), (12, 0, 0, 1, 3), (5, 2, 2, 2, 1), (8, 0, 2, 2, 1), (8, 0, 2, 2, 0), (9, 0, 2, 2, 1),
-    (8, 0, 1, 4, 0), (9, 0, 1, 4, 0), (9, 0, 2, 2, 0), (8, 1, 0, 1, 0), (8, 1, 0, 1, 1), (10, 0, 1),
-    (11, 0, 1, 3), (11, 0, 1, 0), (11, 0, 1, 2), (11, 0, 1, 1), (12, 0, 1, 1, 0), (13, 0, 0, 0), (13, 0, 0, 2),
-    (12, 0, 1, 0, 3), (12, 0, 1, 0, 2), (8, 2, 0, 1, 0), (8, 2, 0, 1, 1), (9, 1, 0, 1, 0), (13, 0, 0, 1),
-    (9, 1, 0, 1, 1), (13, 0, 0, 3), (5, 2, 2, 3, 0), (7, 1), (9, 1, 1, 0, 0), (12, 0, 1, 0, 0),
-    (12, 0, 1, 1, 3), (12, 0, 1, 1, 1), (12, 0, 1, 1, 2), (8, 0, 2, 3, 1), (8, 1, 0, 2, 1), (9, 0, 2, 3, 1),
+    (4, 0, 2), (2, 1, 0, 1, 1), (5, 0, 2, 0, 0), (3, 1, 0, 0), (5, 0, 2, 0, 1), (5, 1, 1, 2, 0),
+    (5, 1, 2, 0, 0), (5, 1, 2, 0, 1), (5, 0, 1, 2, 0), (1, 1, 1, 3), (5, 1, 1, 2, 1), (2, 1, 0, 1, 2),
+    (1, 1, 1, 1), (2, 1, 1, 1, 0), (2, 1, 0, 0, 2), (5, 0, 1, 2, 1), (2, 1, 1, 0, 0), (3, 1, 0, 3), (6, 0),
+    (1, 1, 1, 2), (0, 1, 2), (3, 1, 0, 1), (9, 0, 0, 0, 0), (5, 0, 2, 1, 1), (5, 1, 1, 3, 0), (5, 0, 2, 1, 0),
+    (2, 1, 1, 1, 3), (2, 1, 1, 0, 3), (5, 1, 2, 1, 1), (2, 1, 1, 0, 1), (5, 1, 2, 1, 0), (3, 1, 0, 2),
+    (3, 1, 1, 0), (2, 1, 1, 1, 1), (5, 0, 1, 3, 0), (4, 1, 0), (5, 2, 0, 0, 1), (8, 0, 0, 1, 0),
+    (5, 2, 0, 0, 0), (2, 1, 1, 1, 2), (9, 0, 0, 1, 0), (1, 1, 2, 3), (2, 1, 1, 0, 2), (8, 0, 0, 1, 1),
+    (9, 0, 0, 1, 1), (1, 1, 2, 1), (2, 1, 2, 1, 0), (3, 1, 1, 3), (2, 1, 2, 0, 0), (5, 0, 2, 2, 1),
+    (3, 1, 1, 1), (5, 0, 2, 2, 0), (1, 1, 2, 2), (5, 1, 2, 2, 1), (5, 1, 2, 2, 0), (6, 1), (3, 1, 1, 2),
+    (5, 2, 0, 1, 1), (2, 1, 2, 1, 3), (2, 1, 2, 0, 3), (9, 0, 1, 0, 0), (8, 0, 0, 2, 1), (9, 0, 0, 2, 1),
+    (2, 1, 2, 0, 1), (8, 0, 0, 2, 0), (4, 1, 1), (3, 1, 2, 0), (5, 2, 0, 1, 0), (2, 1, 2, 1, 1),
+    (2, 1, 2, 1, 2), (9, 0, 0, 2, 0), (2, 1, 2, 0, 2), (5, 2, 1, 0, 1), (5, 2, 1, 0, 0), (5, 0, 2, 3, 0),
+    (8, 0, 1, 1, 1), (9, 0, 1, 1, 1), (5, 1, 2, 3, 0), (3, 1, 2, 3), (8, 0, 1, 1, 0), (9, 0, 1, 1, 0),
+    (5, 2, 0, 2, 1), (3, 1, 2, 1), (3, 1, 2, 2), (8, 0, 0, 3, 0), (9, 0, 0, 3, 0), (8, 0, 0, 3, 1),
+    (9, 0, 0, 3, 1), (5, 2, 1, 1, 1), (4, 1, 2), (5, 2, 0, 2, 0), (5, 2, 2, 0, 0), (8, 0, 1, 2, 1),
+    (5, 2, 1, 1, 0), (9, 0, 1, 2, 1), (5, 2, 2, 0, 1), (6, 2), (8, 0, 1, 2, 0), (9, 0, 1, 2, 0),
+    (5, 2, 1, 2, 1), (9, 0, 2, 0, 0), (8, 0, 0, 4, 0), (9, 0, 0, 4, 0), (8, 0, 1, 3, 1), (9, 0, 1, 3, 1),
+    (5, 2, 0, 3, 0), (5, 2, 2, 1, 1), (5, 2, 2, 1, 0), (10, 0, 0), (11, 0, 0, 1), (11, 0, 0, 2), (11, 0, 0, 3),
+    (11, 0, 0, 0), (12, 0, 0, 1, 0), (12, 0, 0, 1, 1), (12, 0, 0, 0, 2), (12, 0, 0, 0, 3), (5, 2, 1, 2, 0),
+    (8, 0, 2, 1, 1), (9, 0, 2, 1, 1), (8, 0, 2, 1, 0), (9, 0, 2, 1, 0), (8, 0, 1, 3, 0), (9, 0, 1, 3, 0),
+    (7, 0), (9, 1, 0, 0, 0), (12, 0, 0, 0, 1), (12, 0, 0, 1, 2), (5, 2, 2, 2, 0), (5, 2, 2, 2, 1),
+    (12, 0, 0, 1, 3), (12, 0, 0, 0, 0), (5, 2, 1, 3, 0), (8, 0, 2, 2, 1), (9, 0, 2, 2, 1), (8, 0, 1, 4, 0),
+    (9, 0, 1, 4, 0), (8, 0, 2, 2, 0), (9, 0, 2, 2, 0), (8, 1, 0, 1, 1), (8, 1, 0, 1, 0), (10, 0, 1),
+    (11, 0, 1, 0), (11, 0, 1, 2), (11, 0, 1, 1), (11, 0, 1, 3), (12, 0, 1, 1, 1), (12, 0, 1, 1, 0),
+    (13, 0, 0, 1), (13, 0, 0, 2), (12, 0, 1, 0, 3), (12, 0, 1, 0, 2), (8, 2, 0, 1, 0), (9, 1, 0, 1, 0),
+    (13, 0, 0, 3), (13, 0, 0, 0), (8, 2, 0, 1, 1), (9, 1, 0, 1, 1), (5, 2, 2, 3, 0), (7, 1), (9, 1, 1, 0, 0),
+    (12, 0, 1, 1, 2), (12, 0, 1, 0, 0), (8, 0, 2, 3, 1), (9, 0, 2, 3, 1), (8, 1, 0, 2, 1), (12, 0, 1, 1, 3),
     (12, 0, 1, 0, 1), (8, 0, 2, 3, 0), (9, 0, 2, 3, 0), (8, 1, 0, 2, 0), (8, 2, 0, 2, 1), (9, 1, 0, 2, 1),
-    (8, 2, 0, 2, 0), (9, 1, 0, 2, 0), (8, 1, 1, 1, 1), (7, 2), (14, 0, 0), (8, 2, 1, 1, 1), (8, 1, 1, 1, 0),
-    (13, 0, 1, 3), (9, 1, 1, 1, 1), (13, 0, 1, 0), (8, 2, 1, 1, 0), (13, 0, 1, 1), (13, 0, 1, 2),
+    (8, 2, 0, 2, 0), (9, 1, 0, 2, 0), (8, 1, 1, 1, 1), (7, 2), (14, 0, 0), (8, 1, 1, 1, 0), (8, 2, 1, 1, 1),
+    (13, 0, 1, 2), (13, 0, 1, 0), (9, 1, 1, 1, 1), (8, 2, 1, 1, 0), (13, 0, 1, 1), (13, 0, 1, 3),
     (8, 1, 0, 3, 1), (9, 1, 1, 1, 0), (9, 1, 2, 0, 0), (8, 2, 0, 3, 1), (9, 1, 0, 3, 1), (8, 0, 2, 4, 0),
-    (8, 1, 1, 2, 1), (9, 0, 2, 4, 0), (8, 1, 0, 3, 0), (15, 2), (8, 2, 0, 3, 0), (9, 1, 0, 3, 0),
-    (8, 1, 2, 1, 0), (8, 1, 2, 1, 1), (10, 0, 2), (11, 0, 2, 2), (11, 0, 2, 1), (11, 0, 2, 3), (8, 2, 1, 2, 1),
-    (9, 1, 1, 2, 1), (14, 0, 1), (8, 1, 1, 3, 1), (11, 0, 2, 0), (12, 0, 2, 1, 0), (12, 0, 2, 0, 3),
-    (8, 1, 1, 2, 0), (12, 0, 2, 0, 2), (8, 2, 2, 1, 0), (9, 1, 2, 1, 0), (8, 2, 1, 2, 0), (9, 1, 1, 2, 0),
-    (8, 1, 0, 4, 0), (12, 0, 2, 1, 1), (8, 2, 2, 1, 1), (9, 1, 2, 1, 1), (8, 2, 0, 4, 0), (9, 1, 0, 4, 0),
-    (8, 1, 2, 2, 1), (12, 0, 2, 0, 1), (12, 0, 2, 1, 2), (8, 1, 2, 2, 0), (8, 2, 1, 3, 1), (9, 1, 1, 3, 1),
-    (8, 1, 1, 3, 0), (12, 0, 2, 1, 3), (12, 0, 2, 0, 0), (8, 2, 2, 2, 0), (9, 1, 2, 2, 0), (10, 1, 0),
-    (11, 1, 0, 1), (11, 1, 0, 3), (11, 1, 0, 0), (11, 1, 0, 2), (12, 1, 0, 1, 0), (12, 1, 0, 0, 2),
-    (12, 1, 0, 0, 3), (12, 1, 0, 1, 1), (8, 2, 1, 3, 0), (9, 1, 1, 3, 0), (8, 2, 2, 2, 1), (9, 1, 2, 2, 1),
-    (8, 1, 2, 3, 1), (8, 1, 2, 3, 0), (13, 0, 2, 2), (13, 0, 2, 1), (8, 1, 1, 4, 0), (8, 2, 2, 3, 0),
-    (9, 1, 2, 3, 0), (13, 0, 2, 3), (13, 0, 2, 0), (8, 2, 1, 4, 0), (9, 1, 1, 4, 0), (12, 1, 0, 1, 3),
+    (8, 1, 1, 2, 1), (9, 0, 2, 4, 0), (8, 1, 0, 3, 0), (15, 2), (8, 2, 0, 3, 0), (9, 1, 0, 3, 0), (14, 0, 1),
+    (8, 1, 2, 1, 1), (8, 1, 2, 1, 0), (10, 0, 2), (11, 0, 2, 0), (11, 0, 2, 2), (8, 2, 1, 2, 1),
+    (9, 1, 1, 2, 1), (11, 0, 2, 3), (8, 1, 1, 3, 1), (11, 0, 2, 1), (12, 0, 2, 1, 0), (12, 0, 2, 0, 3),
+    (8, 1, 1, 2, 0), (12, 0, 2, 0, 2), (12, 0, 2, 1, 1), (8, 2, 2, 1, 0), (9, 1, 2, 1, 0), (8, 2, 1, 2, 0),
+    (8, 1, 0, 4, 0), (9, 1, 1, 2, 0), (8, 2, 2, 1, 1), (9, 1, 2, 1, 1), (8, 2, 0, 4, 0), (9, 1, 0, 4, 0),
+    (8, 1, 2, 2, 1), (8, 1, 2, 2, 0), (12, 0, 2, 0, 0), (12, 0, 2, 1, 2), (8, 2, 1, 3, 1), (9, 1, 1, 3, 1),
+    (8, 1, 1, 3, 0), (12, 0, 2, 1, 3), (12, 0, 2, 0, 1), (8, 2, 2, 2, 0), (9, 1, 2, 2, 0), (10, 1, 0),
+    (11, 1, 0, 1), (11, 1, 0, 3), (11, 1, 0, 0), (11, 1, 0, 2), (12, 1, 0, 0, 2), (12, 1, 0, 1, 1),
+    (12, 1, 0, 1, 0), (12, 1, 0, 0, 3), (8, 2, 1, 3, 0), (9, 1, 1, 3, 0), (8, 2, 2, 2, 1), (9, 1, 2, 2, 1),
+    (8, 1, 2, 3, 1), (8, 1, 2, 3, 0), (13, 0, 2, 0), (8, 1, 1, 4, 0), (13, 0, 2, 2), (8, 2, 2, 3, 0),
+    (9, 1, 2, 3, 0), (13, 0, 2, 1), (13, 0, 2, 3), (8, 2, 1, 4, 0), (9, 1, 1, 4, 0), (12, 1, 0, 1, 3),
     (12, 1, 0, 0, 1), (12, 1, 0, 0, 0), (12, 1, 0, 1, 2), (8, 2, 2, 3, 1), (9, 1, 2, 3, 1), (8, 1, 2, 4, 0),
-    (10, 1, 1), (11, 1, 1, 3), (11, 1, 1, 0), (11, 1, 1, 2), (11, 1, 1, 1), (12, 1, 1, 1, 0), (12, 1, 1, 1, 1),
-    (12, 1, 1, 0, 2), (12, 1, 1, 0, 3), (8, 2, 2, 4, 0), (9, 1, 2, 4, 0), (13, 1, 0, 3), (10, 1, 2),
-    (11, 1, 2, 2), (11, 1, 2, 0), (11, 1, 2, 1), (11, 1, 2, 3), (13, 1, 0, 1), (13, 1, 0, 2), (12, 1, 2, 0, 2),
-    (12, 1, 2, 1, 0), (12, 1, 2, 1, 1), (12, 1, 2, 0, 3), (12, 1, 1, 1, 3), (14, 0, 2), (13, 1, 0, 0),
-    (12, 1, 1, 1, 2), (12, 1, 1, 0, 0), (12, 1, 1, 0, 1), (12, 1, 2, 1, 2), (12, 1, 2, 0, 0), (15, 1),
-    (12, 1, 2, 0, 1), (12, 1, 2, 1, 3), (15, 0), (13, 1, 1, 2), (13, 1, 1, 3), (14, 1, 0), (13, 1, 2, 2),
-    (13, 1, 1, 0), (13, 1, 1, 1), (13, 1, 2, 0), (13, 1, 2, 1), (13, 1, 2, 3), (14, 1, 1), (14, 1, 2),
+    (10, 1, 1), (11, 1, 1, 1), (11, 1, 1, 0), (11, 1, 1, 2), (11, 1, 1, 3), (12, 1, 1, 0, 3), (12, 1, 1, 1, 1),
+    (12, 1, 1, 1, 0), (12, 1, 1, 0, 2), (8, 2, 2, 4, 0), (9, 1, 2, 4, 0), (13, 1, 0, 3), (14, 0, 2),
+    (10, 1, 2), (11, 1, 2, 0), (11, 1, 2, 2), (11, 1, 2, 1), (13, 1, 0, 1), (13, 1, 0, 2), (11, 1, 2, 3),
+    (12, 1, 2, 0, 3), (12, 1, 2, 0, 2), (12, 1, 2, 1, 1), (13, 1, 0, 0), (12, 1, 2, 1, 0), (12, 1, 1, 1, 2),
+    (12, 1, 1, 0, 1), (12, 1, 1, 1, 3), (12, 1, 1, 0, 0), (12, 1, 2, 1, 2), (12, 1, 2, 0, 0), (15, 0),
+    (12, 1, 2, 0, 1), (12, 1, 2, 1, 3), (15, 1), (13, 1, 1, 2), (13, 1, 1, 3), (14, 1, 0), (13, 1, 2, 2),
+    (13, 1, 1, 1), (13, 1, 1, 0), (13, 1, 2, 0), (13, 1, 2, 1), (13, 1, 2, 3), (14, 1, 1), (14, 1, 2),
 )
 
 

time: 111 us -> 112 us (level)
    pallas_call x1, Pallas kernels: 107 us -> 108 us  [per_device(): pl.pallas_call(kernel, out_shape=(pltpu.VMEM((128, 512), BF16), pltpu.VME...]
where the time goes in v5:
time: 112 us; the launch traced here: 111 us
  Pallas kernels  110 us (98%)
    pallas_call x1, Pallas kernels, per_device(): pl.pallas_call(kernel, out_shape=(pltpu.VMEM((128, 512), BF16), pltpu.VME...  108 us

profile of v5, /device:TPU:1, one launch (start us, length us, event | category | flops | bytes accessed | tf_op | source)
XLA Modules:
  0.0 111.0 jit_solution(18214938552682432329)
XLA Ops:
  0.6 108.3 %slab.1 = (bf16[128,512]{1,0:T(8,128)(2,1)S(1)}, bf16[128,512]{1,0:T(8,128)(2,1)S(1)}, f32[1024,256]{1,0:T(8,128)S(1)}, f32[1024,256]{1,0:T(8,128)S(1)}, f32[1024,256]{1,0:T(8,128)S(1)}) custom-call(bf16[128,512]{1,0:T(8,128)(2,1)} %tok.1, bf16[1024,256]{1,0:T(8,128)(2,1)} %wg.1, bf16[1024,256]{1,0:T(8,128)(2,1)} %wu.1, bf16[1024,256]{1,0:T(8,128)(2,1)} %wd.1, ...), custom_call_target="tpu_custom_call" | custom-call | tf_op jit(solution)/shard_map/slab/pallas_call | solution.py:399
  108.9 1.9 %put_out.1 = (bf16[128,512]{1,0:T(8,128)(2,1)}, bf16[128,512]{1,0:T(8,128)(2,1)}, f32[1024,256]{1,0:T(8,128)}, f32[1024,256]{1,0:T(8,128)}, f32[1024,256]{1,0:T(8,128)}) custom-call(bf16[128,512]{1,0:T(8,128)(2,1)S(1)} %get-tuple-element.10.refs_0_, bf16[128,512]{1,0:T(8,128)(2,1)S(1)} %get-tuple-element.11.refs_1_, ...), custom_call_target="tpu_custom_call" | custom-call | tf_op jit(solution)/shard_map/put_out/pallas_call | solution.py:449
